TPU v7x, 256 devices: a whole 4x4x8 slice. The times are simulated.
256 devices in a mesh: stream: 8 (over z_lo, core), azim: 32 (over z_hi, x, y).
Axes of the slice: x: 4, y: 4, z: 8 (z_hi: 2, z_lo: 4; z = z_hi * 4 + z_lo), core: 2. Of those that a mesh axis runs over, the one named last changes fastest.
Arguments:
- surface_signal: bfloat16 [64, 524288], P(None, ('stream', 'azim')), may hold values from -6 to 6
- retarded_weights: bfloat16 [4096, 64, 64], P(('stream', 'azim')), may hold values from -0.75 to 0.75
- radiation_weights: bfloat16 [1024, 524288], P(None, ('stream', 'azim')), may hold values from -0.03125 to 0.03125
- target_signal: float32 [64, 1024], replicated, may hold values from -6 to 6
- observer_weights: float32 [1024], replicated, may hold values from 0.5 to 2
- sample_weights: float32 [64], replicated, may hold values from 1 to 8
- host_element: int32 [524288], P(('stream', 'azim')), may hold values from 0 to 4095
- source_profile: float32 [320], replicated, may hold values from -6 to 6
- adjoint_state: bfloat16 [320, 32, 128, 256], P(None, 'stream', 'azim'), may hold values from -6 to 6
- volume_operator: bfloat16 [320, 320], replicated, may hold values from -0.3125 to 0.3125
- lift_operator: bfloat16 [320, 480], replicated, may hold values from -0.25 to 0.25
Outputs:
- obs_sens: float32 [64, 1024], P(None, 'azim')
- adjoint_next: float32 [320, 32, 128, 256], P(None, 'stream', 'azim')
Inputs may be any that keep to these rules, and one draw needn't show every extreme that they name: host_element[i] numbers an element among the 4 x 4 x 256 elements of the device block that holds surface point i, as (x 4 + a) * 256 + r in that block.
All inputs are finite; a program needn't handle non-finite values.
Results may differ from a plain program's by a relative error of at most 0.0039.
Values may be sent and summed in bfloat16 or wider, within the bound.
A program may use at most 64 MiB of HBM per device.

v0:
```python
import jax
import jax.numpy as jnp
from jax import lax
from jax.sharding import PartitionSpec as P

NVAR = 5
NODE = 4


def cut_along(shard, dim, devices):
    before, after = (shard.shape[:dim], shard.shape[dim + 1 :])
    return jnp.moveaxis(shard.reshape(*before, devices, -1, *after), dim, 0)


def summed_on_arrival(shard, axis, dim):
    tiles = cut_along(shard, dim, lax.axis_size(axis))
    arrived = lax.all_to_all(tiles, axis, split_axis=0, concat_axis=0, tiled=True)
    return arrived.sum(axis=0)


def copy_for_each(shard, axis):
    copies = jnp.broadcast_to(shard, (lax.axis_size(axis), *shard.shape))
    return lax.all_to_all(copies, axis, split_axis=0, concat_axis=0, tiled=True)


def over_copies(shard, axis):
    everything = copy_for_each(shard, axis)
    return jnp.sum(everything, axis=0)


def in_order(tiles, dim):
    tiles = jnp.moveaxis(tiles, 0, dim)
    dims = tiles.shape
    return tiles.reshape(*dims[:dim], dims[dim] * dims[dim + 1], *dims[dim + 2 :])


def collect(shard, axis, dim):
    tiles = copy_for_each(shard, axis)
    return in_order(tiles, dim)


def extended(block, sides, width, periodic):
    for axis, dim in sides:
        count = lax.axis_size(axis)
        forward = [(i, i + 1) for i in range(count - 1)]
        if periodic:
            forward.append((count - 1, 0))
        backward = [(target, source) for source, target in forward]
        low = lax.ppermute(
            lax.slice_in_dim(block, block.shape[dim] - width, None, axis=dim), axis, forward
        )
        high = lax.ppermute(lax.slice_in_dim(block, 0, width, axis=dim), axis, backward)
        block = jnp.concatenate([low, block, high], axis=dim)
    return block


def hann_taper(count):
    samples = jnp.arange(count, dtype=jnp.float32)
    return 0.5 - 0.5 * jnp.cos(2.0 * jnp.pi * (samples + 0.5) / count)


def face_traces(state):
    rest = state.shape[1:]
    faces = NVAR * NODE * NODE
    shaped = state.reshape((NVAR, NODE, NODE, NODE) + rest)
    lower_axial = shaped[:, 0].reshape((faces,) + rest)
    upper_axial = shaped[:, NODE - 1].reshape((faces,) + rest)
    lower_sector = shaped[:, :, 0].reshape((faces,) + rest)
    upper_sector = shaped[:, :, NODE - 1].reshape((faces,) + rest)
    lower_radial = shaped[:, :, :, 0].reshape((faces,) + rest)
    upper_radial = shaped[:, :, :, NODE - 1].reshape((faces,) + rest)
    return (lower_axial, upper_axial, lower_sector, upper_sector, lower_radial, upper_radial)


def body(
    surface_signal,
    retarded_weights,
    radiation_weights,
    target_signal,
    observer_weights,
    sample_weights,
    host_element,
    source_profile,
    adjoint_state,
    volume_operator,
    lift_operator,
):
    window = surface_signal.shape[0]
    points = surface_signal.shape[1]
    blocks = retarded_weights.shape[0]
    observers = radiation_weights.shape[0]
    tapering = hann_taper(window)
    blocked = surface_signal.reshape(window, blocks, points // blocks)
    delayed = jnp.einsum(
        "bkt,kbs->tbs", retarded_weights, blocked, preferred_element_type=jnp.float32
    )
    delayed_low = delayed.astype(jnp.bfloat16).reshape(window, points)
    partial_value = lax.dot_general(
        delayed_low, radiation_weights, (((1,), (1,)), ((), ())), preferred_element_type=jnp.float32
    )
    sectors = lax.axis_size("azim")
    sector = lax.axis_index("azim")
    own_width = observers // sectors
    own_sums = summed_on_arrival(partial_value, "azim", 1)
    own_sums = over_copies(own_sums, "stream")
    weights_own = lax.dynamic_slice_in_dim(observer_weights, sector * own_width, own_width, 0)
    target_own = lax.dynamic_slice_in_dim(target_signal, sector * own_width, own_width, 1)
    sens_own = weights_own[None, :] * tapering[:, None] * (own_sums - target_own)
    sens_low = collect(sens_own.astype(jnp.bfloat16), "azim", 1)
    spread = jnp.dot(sens_low, radiation_weights, preferred_element_type=jnp.float32)
    spread_low = spread.astype(jnp.bfloat16).reshape(window, blocks, points // blocks)
    source_time = jnp.einsum(
        "bkt,tbs->kbs", retarded_weights, spread_low, preferred_element_type=jnp.float32
    )
    strength = jnp.sum(source_time * sample_weights[:, None, None], axis=0).reshape(points)
    components = adjoint_state.shape[0]
    elements = adjoint_state.shape[1] * adjoint_state.shape[2] * adjoint_state.shape[3]
    element_source = jax.ops.segment_sum(strength, host_element, num_segments=elements)
    lower_axial, upper_axial, lower_sector, upper_sector, lower_radial, upper_radial = face_traces(
        adjoint_state
    )
    packed_axial = jnp.concatenate([lower_axial[:, :1], upper_axial[:, 1:]], axis=1)
    padded_axial = extended(packed_axial, (("stream", 1),), 1, False)
    from_lower_axial = jnp.concatenate([padded_axial[:, :1], upper_axial[:, :-1]], axis=1)
    from_upper_axial = jnp.concatenate([lower_axial[:, 1:], padded_axial[:, -1:]], axis=1)
    packed_sector = jnp.concatenate([lower_sector[:, :, :1], upper_sector[:, :, 1:]], axis=2)
    padded_sector = extended(packed_sector, (("azim", 2),), 1, True)
    from_lower_sector = jnp.concatenate([padded_sector[:, :, :1], upper_sector[:, :, :-1]], axis=2)
    from_upper_sector = jnp.concatenate([lower_sector[:, :, 1:], padded_sector[:, :, -1:]], axis=2)
    zero_rim = jnp.zeros_like(upper_radial[..., :1])
    from_lower_radial = jnp.concatenate([zero_rim, upper_radial[..., :-1]], axis=3)
    from_upper_radial = jnp.concatenate([lower_radial[..., 1:], zero_rim], axis=3)
    stacked = jnp.concatenate(
        [
            from_lower_axial,
            from_upper_axial,
            from_lower_sector,
            from_upper_sector,
            from_lower_radial,
            from_upper_radial,
        ],
        axis=0,
    ).reshape(-1, elements)
    flat_state = adjoint_state.reshape(components, elements)
    volume_term = jnp.dot(volume_operator, flat_state, preferred_element_type=jnp.float32)
    face_term = jnp.dot(lift_operator, stacked, preferred_element_type=jnp.float32)
    updated = (
        flat_state.astype(jnp.float32)
        + volume_term
        + face_term
        + source_profile[:, None] * element_source[None, :]
    )
    return (sens_own, updated.reshape(adjoint_state.shape))


def solution(mesh):
    return jax.shard_map(
        body,
        mesh=mesh,
        in_specs=(
            P(None, ("stream", "azim")),
            P(("stream", "azim"), None, None),
            P(None, ("stream", "azim")),
            P(),
            P(),
            P(),
            P(("stream", "azim")),
            P(),
            P(None, "stream", "azim", None),
            P(),
            P(),
        ),
        out_specs=(P(None, "azim"), P(None, "stream", "azim", None)),
        check_vma=False,
    )
```

profile of v0, /device:TPU:1, one launch (start us, length us, event | category | flops | bytes accessed | tf_op | source)
XLA Modules:
  0.0 136.0 jit_solution(670365097451050993)
XLA Ops:
  3.0 3.6 %fusion.15 = f32[32,32,64]{2,1,0:T(8,128)S(1)} fusion(bf16[64,2048,1]{1,0,2:T(8,128)(2,1)} %reshape.63, bf16[32,32,2048]{2,1,0:T(8,128)(2,1)} %bitcast.55), kind=kOutput, calls=%fused_computation.31 | convolution fusion | flops 268435456 | bytes 4718592 | tf_op jit(solution)/shard_map/dot_general | solution.py:98
  7.7 14.6 %all-to-all-start = ((f32[32,1,2048]{2,1,0:T(1,128)}), f32[32,1,2048]{2,1,0:T(1,128)}, u32[]{:S(2)}, u32[]{:S(2)}) async-start(f32[32,1,2048]{2,1,0:T(1,128)} %reshape.67), calls=%async_computation | async-start | bytes 524288 | tf_op jit(solution)/shard_map/all_to_all | solution.py:17
  23.8 3.5 %collective-permute-start = (bf16[80,1,4,256]{3,2,1,0:T(4,128)(2,1)}, bf16[80,1,4,256]{3,2,1,0:T(4,128)(2,1)}, u32[]{:S(2)}, u32[]{:S(2)}) collective-permute-start(bf16[80,1,4,256]{3,2,1,0:T(4,128)(2,1)} %slice.69), channel_id=1, source_target_pairs={{0,32},{32,64},{64,96},{96,128},{128,160},{160,192},{192,224},{1,3... | collective-permute-start | bytes 491528 | tf_op jit(solution)/shard_map/ppermute | solution.py:49
  28.0 1.9 %collective-permute-start.1 = (bf16[80,1,4,256]{3,2,1,0:T(4,128)(2,1)}, bf16[80,1,4,256]{3,2,1,0:T(4,128)(2,1)}, u32[]{:S(2)}, u32[]{:S(2)}) collective-permute-start(bf16[80,1,4,256]{3,2,1,0:T(4,128)(2,1)} %slice.73), channel_id=1, source_target_pairs={{32,0},{64,32},{96,64},{128,96},{160,128},{192,160},{224,192},{33,... | collective-permute-start | bytes 491528 | tf_op jit(solution)/shard_map/ppermute | solution.py:52
  34.8 8.2 %collective-permute-start.3 = (bf16[80,4,1,256]{3,2,1,0:T(2,128)(2,1)}, bf16[80,4,1,256]{3,2,1,0:T(2,128)(2,1)}, u32[]{:S(2)}, u32[]{:S(2)}) collective-permute-start(bf16[80,4,1,256]{3,2,1,0:T(2,128)(2,1)} %slice.79), channel_id=1, source_target_pairs={{1,0},{2,1},{3,2},{4,3},{5,4},{6,5},{7,6},{8,7},{9,8},{10,9},{11,1... | collective-permute-start | bytes 491528 | tf_op jit(solution)/shard_map/ppermute | solution.py:52
  43.0 1.9 %fusion.12 = (bf16[5,4,4,1,4,4,256]{6,5,4,3,2,1,0:T(4,128)(2,1)}, bf16[5,4,4,1,4,4,256]{6,5,4,3,2,1,0:T(4,128)(2,1)}) fusion(bf16[5,4,4,4,4,4,256]{6,5,4,3,2,1,0:T(4,128)(2,1)S(1)} %bitcast.58), kind=kLoop, calls=%fused_computation.28 | loop fusion | bytes 2621440 | tf_op jit(solution)/shard_map/slice | solution.py:70
  45.8 2.0 %slice.70 = bf16[80,3,4,256]{3,2,1,0:T(4,128)(2,1)} slice(bf16[80,4,4,256]{3,2,1,0:T(4,128)(2,1)} %bitcast.67), slice={[0:80], [0:3], [0:4], [0:256]} | slice | bytes 983040 | tf_op jit(solution)/shard_map/slice | solution.py:124
  49.0 2.3 %slice.78 = bf16[80,4,3,256]{3,2,1,0:T(4,128)(2,1)} slice(bf16[80,4,4,256]{3,2,1,0:T(4,128)(2,1)} %bitcast.62), slice={[0:80], [0:4], [1:4], [0:256]} | slice | bytes 983040 | tf_op jit(solution)/shard_map/slice | solution.py:129
  51.3 3.5 %reshape.47 = bf16[320,4096]{1,0:T(8,128)(2,1)} reshape(bf16[320,4,4,256]{3,2,1,0:T(4,128)(2,1)S(1)} %copy-done.1) | data formatting | bytes 5242880 | tf_op jit(solution)/shard_map/reshape | solution.py:144
  55.8 1.6 %slice.83 = bf16[80,4,4,255]{3,2,1,0:T(4,128)(2,1)S(1)} slice(bf16[80,4,4,256]{3,2,1,0:T(4,128)(2,1)} %bitcast.68), slice={[0:80], [0:4], [0:4], [1:256]} | slice | bytes 1305600 | tf_op jit(solution)/shard_map/slice | solution.py:132
  57.4 2.2 %maximum_dynamic-update-slice_fusion.3 = bf16[480,4,4,256]{3,2,1,0:T(4,128)(2,1)} fusion(bf16[80,3,4,256]{3,2,1,0:T(4,128)(2,1)} %slice.70, bf16[80,1,4,256]{3,2,1,0:T(4,128)(2,1)} %collective-permute-done), kind=kLoop, calls=%fused_computation.15 | loop fusion | flops 1310719 | bytes 1310720
  59.6 2.1 %maximum_dynamic-update-slice_fusion.2 = bf16[480,4,4,256]{3,2,1,0:T(4,128)(2,1)} fusion(bf16[480,4,4,256]{3,2,1,0:T(4,128)(2,1)} %maximum_dynamic-update-slice_fusion.3, bf16[80,1,4,256]{3,2,1,0:T(4,128)(2,1)} %collective-permute-done.1, bf16[80,3,4,256]{3,2,1,0:T(4,128)(2,1)S(1)} %slice.72), kind=kLoop, calls=%fused_computation.14 | loop fusion | flops 1310720 | bytes 1310720
  61.7 2.5 %maximum_dynamic-update-slice_fusion.1 = bf16[480,4,4,256]{3,2,1,0:T(4,128)(2,1)} fusion(bf16[480,4,4,256]{3,2,1,0:T(4,128)(2,1)} %maximum_dynamic-update-slice_fusion.2, bf16[80,4,3,256]{3,2,1,0:T(4,128)(2,1)S(1)} %bitcast.60, bf16[80,4,1,256]{3,2,1,0:T(2,128)(2,1)} %collective-permute-done.2), kind=kLoop, calls=%fused_computation.13 | loop fusion | flops 1310720 | bytes 1474560
  64.2 2.5 %maximum_dynamic-update-slice_fusion = bf16[480,4,4,256]{3,2,1,0:T(4,128)(2,1)} fusion(bf16[480,4,4,256]{3,2,1,0:T(4,128)(2,1)} %maximum_dynamic-update-slice_fusion.1, bf16[80,4,1,256]{3,2,1,0:T(2,128)(2,1)} %collective-permute-done.3, bf16[80,4,3,256]{3,2,1,0:T(4,128)(2,1)S(1)} %copy-done.8), kind=kLoop, calls=%fused_computation.12 | loop fusion | flops 1310720 | bytes 1474560
  68.6 2.2 %reduce.1 = f32[32,2048]{1,0:T(8,128)S(1)} reduce(f32[32,1,2048]{2,1,0:T(1,128)} %all-to-all-done, f32[]{:T(128)} %broadcast.33), dimensions={1}, to_apply=%all_to_all.9.reduce_sub_computation | reduce | bytes 524292 | tf_op jit(solution)/shard_map/all_to_all | solution.py:17
  71.8 4.8 %all-to-all-start.1 = ((f32[8,1,2048]{2,1,0:T(1,128)}), f32[8,1,2048]{2,1,0:T(1,128)S(1)}, u32[]{:S(2)}, u32[]{:S(2)}) async-start(f32[8,1,2048]{2,1,0:T(1,128)} %reshape.69), calls=%async_computation.1 | async-start | bytes 131072 | tf_op jit(solution)/shard_map/all_to_all | solution.py:23
  77.8 7.8 %reshape.49 = bf16[480,4096]{1,0:T(8,128)(2,1)} reshape(bf16[480,4,4,256]{3,2,1,0:T(4,128)(2,1)} %pad_dynamic-update-slice_fusion) | data formatting | bytes 7864320 | tf_op jit(solution)/shard_map/reshape | solution.py:143
  88.1 7.0 %all-to-all-start.2 = ((bf16[32,2,1024]{2,1,0:T(2,128)(2,1)}), bf16[32,2,1024]{2,1,0:T(2,128)(2,1)S(1)}, u32[]{:S(2)}, u32[]{:S(2)}) async-start(bf16[32,2,1024]{2,1,0:T(2,128)(2,1)} %reshape.71), calls=%async_computation.2 | async-start | bytes 262144 | tf_op jit(solution)/shard_map/all_to_all | solution.py:23
  95.1 6.0 %convolution_bitcast_fusion = f32[320,4096]{1,0:T(8,128)} fusion(bf16[320,480]{1,0:T(8,128)(2,1)S(1)} %copy-done, bf16[480,4096]{1,0:T(8,128)(2,1)} %reshape.49), kind=kOutput, calls=%fused_computation.1 | convolution fusion | flops 1258291200 | bytes 9482240 | tf_op jit(solution)/shard_map/dot_general | solution.py:146
  101.1 5.4 %all-to-all-done.2 = bf16[32,2,1024]{2,1,0:T(2,128)(2,1)S(1)} async-done(((bf16[32,2,1024]{2,1,0:T(2,128)(2,1)}), bf16[32,2,1024]{2,1,0:T(2,128)(2,1)S(1)}, u32[]{:S(2)}, u32[]{:S(2)}) %all-to-all-start.2) | async-done | bytes 131104 | tf_op jit(solution)/shard_map/all_to_all | solution.py:23
  106.8 3.1 %fusion.4 = bf16[8,16,8,128]{3,2,1,0:T(8,128)(2,1)S(1)} fusion(bf16[64,1024]{0,1:T(8,128)(2,1)S(1)} %bitcast.69, bf16[1024,2048]{1,0:T(8,128)(2,1)} %param.13), kind=kOutput, calls=%fused_computation.11 | convolution fusion | flops 268566528 | bytes 4587520 | tf_op jit(solution)/shard_map/dot_general | solution.py:110
  110.1 11.6 %scatter_custom_fusion = f32[4096]{0:T(1024)S(1)} fusion(s32[2048]{0:T(1024)} %param.17, f32[2048]{0:T(1024)S(1)} %bitcast.70, f32[]{:T(128)} %constant.6.clone.1), kind=kCustom, calls=%fused_computation.23 | custom fusion | flops 2048 | bytes 16896 | tf_op jit(solution)/shard_map/scatter-add | solution.py:118
  121.8 6.6 %fusion.1 = f32[320,4096]{1,0:T(8,128)} fusion(f32[320,4096]{1,0:T(8,128)} %convolution_bitcast_fusion, bf16[320,320]{1,0:T(8,128)(2,1)S(1)} %copy-done.11, bf16[320,4096]{1,0:T(8,128)(2,1)S(1)} %copy-done.9, f32[4096]{0:T(1024)S(1)} %scatter_custom_fusion, f32[320]{0:T(512)S(1)} %copy-done.12), kind=kOutput, calls=%fused_computation.4 | convolution fusion | flops 845414400 | bytes 13329664 | tf_op jit(solution)/shard_map/dot_general | solution.py:145
  128.4 7.6 %reshape.53 = f32[320,4,4,256]{3,2,1,0:T(4,128)} reshape(f32[320,4096]{1,0:T(8,128)} %fusion.1) | data formatting | bytes 10485760 | tf_op jit(solution)/shard_map/reshape | solution.py:153
  (65 shorter events, 20.5 us)
Async XLA Ops:
  0.6 94.5 %copy-start = (bf16[320,480]{1,0:T(8,128)(2,1)S(1)}, bf16[320,480]{1,0:T(8,128)(2,1)}, u32[]{:S(2)}) copy-start(bf16[320,480]{1,0:T(8,128)(2,1)} %param.21) | copy-start | bytes 921604
  3.0 19.3 %copy-start.1 = (bf16[320,4,4,256]{3,2,1,0:T(4,128)(2,1)S(1)}, bf16[320,4,4,256]{3,2,1,0:T(4,128)(2,1)}, u32[]{:S(2)}) copy-start(bf16[320,4,4,256]{3,2,1,0:T(4,128)(2,1)} %param.19) | copy-start | bytes 7864324
  7.7 60.4 %all-to-all-start = ((f32[32,1,2048]{2,1,0:T(1,128)}), f32[32,1,2048]{2,1,0:T(1,128)}, u32[]{:S(2)}, u32[]{:S(2)}) async-start(f32[32,1,2048]{2,1,0:T(1,128)} %reshape.67), calls=%async_computation | async-start | bytes 524288 | tf_op jit(solution)/shard_map/all_to_all | solution.py:17
  22.9 5.1 %copy-start.6 = (bf16[5,1,4,4,4,4,256]{6,5,4,3,2,1,0:T(4,128)(2,1)}, bf16[5,1,4,4,4,4,256]{6,5,4,3,2,1,0:T(4,128)(2,1)S(1)}, u32[]{:S(2)}) copy-start(bf16[5,1,4,4,4,4,256]{6,5,4,3,2,1,0:T(4,128)(2,1)S(1)} %get-tuple-element.8) | copy-start | bytes 1966084
  22.9 5.1 %copy-start.7 = (bf16[5,1,4,4,4,4,256]{6,5,4,3,2,1,0:T(4,128)(2,1)}, bf16[5,1,4,4,4,4,256]{6,5,4,3,2,1,0:T(4,128)(2,1)S(1)}, u32[]{:S(2)}) copy-start(bf16[5,1,4,4,4,4,256]{6,5,4,3,2,1,0:T(4,128)(2,1)S(1)} %get-tuple-element.9) | copy-start | bytes 1966084
  23.8 33.6 %collective-permute-start = (bf16[80,1,4,256]{3,2,1,0:T(4,128)(2,1)}, bf16[80,1,4,256]{3,2,1,0:T(4,128)(2,1)}, u32[]{:S(2)}, u32[]{:S(2)}) collective-permute-start(bf16[80,1,4,256]{3,2,1,0:T(4,128)(2,1)} %slice.69), channel_id=1, source_target_pairs={{0,32},{32,64},{64,96},{96,128},{128,160},{160,192},{192,224},{1,3... | collective-permute-start | bytes 491528 | tf_op jit(solution)/shard_map/ppermute | solution.py:49
  28.0 31.6 %collective-permute-start.1 = (bf16[80,1,4,256]{3,2,1,0:T(4,128)(2,1)}, bf16[80,1,4,256]{3,2,1,0:T(4,128)(2,1)}, u32[]{:S(2)}, u32[]{:S(2)}) collective-permute-start(bf16[80,1,4,256]{3,2,1,0:T(4,128)(2,1)} %slice.73), channel_id=1, source_target_pairs={{32,0},{64,32},{96,64},{128,96},{160,128},{192,160},{224,192},{33,... | collective-permute-start | bytes 491528 | tf_op jit(solution)/shard_map/ppermute | solution.py:52
  30.5 0.8 copy-start.2
  30.5 3.3 %copy-start.4 = (bf16[5,4,1,4,4,4,256]{6,5,4,3,2,1,0:T(4,128)(2,1)}, bf16[5,4,1,4,4,4,256]{6,5,4,3,2,1,0:T(4,128)(2,1)S(1)}, u32[]{:S(2)}) copy-start(bf16[5,4,1,4,4,4,256]{6,5,4,3,2,1,0:T(4,128)(2,1)S(1)} %get-tuple-element.6) | copy-start | bytes 1966084
  32.4 29.3 %collective-permute-start.2 = (bf16[80,4,1,256]{3,2,1,0:T(2,128)(2,1)}, bf16[80,4,1,256]{3,2,1,0:T(2,128)(2,1)}, u32[]{:S(2)}, u32[]{:S(2)}) collective-permute-start(bf16[80,4,1,256]{3,2,1,0:T(2,128)(2,1)} %slice.75), channel_id=1, source_target_pairs={{0,1},{1,2},{2,3},{3,4},{4,5},{5,6},{6,7},{7,8},{8,9},{9,10},{10,1... | collective-permute-start | bytes 491528 | tf_op jit(solution)/shard_map/ppermute | solution.py:49
  34.8 29.4 %collective-permute-start.3 = (bf16[80,4,1,256]{3,2,1,0:T(2,128)(2,1)}, bf16[80,4,1,256]{3,2,1,0:T(2,128)(2,1)}, u32[]{:S(2)}, u32[]{:S(2)}) collective-permute-start(bf16[80,4,1,256]{3,2,1,0:T(2,128)(2,1)} %slice.79), channel_id=1, source_target_pairs={{1,0},{2,1},{3,2},{4,3},{5,4},{6,5},{7,6},{8,7},{9,8},{10,9},{11,1... | collective-permute-start | bytes 491528 | tf_op jit(solution)/shard_map/ppermute | solution.py:52
  54.9 6.8 %copy-start.3 = (bf16[5,4,1,4,4,4,256]{6,5,4,3,2,1,0:T(4,128)(2,1)S(1)}, bf16[5,4,1,4,4,4,256]{6,5,4,3,2,1,0:T(4,128)(2,1)}, u32[]{:S(2)}) copy-start(bf16[5,4,1,4,4,4,256]{6,5,4,3,2,1,0:T(4,128)(2,1)} %copy-done.2) | copy-start | bytes 1966084
  54.9 9.3 %copy-start.8 = (bf16[80,4,3,256]{3,2,1,0:T(4,128)(2,1)S(1)}, bf16[80,4,3,256]{3,2,1,0:T(4,128)(2,1)}, u32[]{:S(2)}) copy-start(bf16[80,4,3,256]{3,2,1,0:T(4,128)(2,1)} %slice.78) | copy-start | bytes 1474564
  54.9 11.8 %copy-start.5 = (bf16[5,4,4,1,4,4,256]{6,5,4,3,2,1,0:T(4,128)(2,1)S(1)}, bf16[5,4,4,1,4,4,256]{6,5,4,3,2,1,0:T(4,128)(2,1)}, u32[]{:S(2)}) copy-start(bf16[5,4,4,1,4,4,256]{6,5,4,3,2,1,0:T(4,128)(2,1)} %get-tuple-element.5) | copy-start | bytes 1966084
  71.8 13.8 %all-to-all-start.1 = ((f32[8,1,2048]{2,1,0:T(1,128)}), f32[8,1,2048]{2,1,0:T(1,128)S(1)}, u32[]{:S(2)}, u32[]{:S(2)}) async-start(f32[8,1,2048]{2,1,0:T(1,128)} %reshape.69), calls=%async_computation.1 | async-start | bytes 131072 | tf_op jit(solution)/shard_map/all_to_all | solution.py:23
  88.1 18.4 %all-to-all-start.2 = ((bf16[32,2,1024]{2,1,0:T(2,128)(2,1)}), bf16[32,2,1024]{2,1,0:T(2,128)(2,1)S(1)}, u32[]{:S(2)}, u32[]{:S(2)}) async-start(bf16[32,2,1024]{2,1,0:T(2,128)(2,1)} %reshape.71), calls=%async_computation.2 | async-start | bytes 262144 | tf_op jit(solution)/shard_map/all_to_all | solution.py:23
  101.1 8.8 %copy-start.13 = (f32[64]{0:T(128)S(1)}, f32[64]{0:T(128)}, u32[]{:S(2)}) copy-start(f32[64]{0:T(128)} %param.16) | copy-start | bytes 772
  101.1 20.6 %copy-start.9 = (bf16[320,4096]{1,0:T(8,128)(2,1)S(1)}, bf16[320,4096]{1,0:T(8,128)(2,1)}, u32[]{:S(2)}) copy-start(bf16[320,4096]{1,0:T(8,128)(2,1)} %reshape.47) | copy-start | bytes 7864324
  101.1 20.6 %copy-start.12 = (f32[320]{0:T(512)S(1)}, f32[320]{0:T(512)}, u32[]{:S(2)}) copy-start(f32[320]{0:T(512)} %param.18) | copy-start | bytes 3844
  106.7 3.2 %copy-start.10 = (bf16[16,64,64]{2,1,0:T(8,128)(2,1)S(1)}, bf16[16,64,64]{2,1,0:T(8,128)(2,1)}, u32[]{:S(2)}) copy-start(bf16[16,64,64]{2,1,0:T(8,128)(2,1)} %param.12) | copy-start | bytes 393220
  106.8 15.0 %copy-start.11 = (bf16[320,320]{1,0:T(8,128)(2,1)S(1)}, bf16[320,320]{1,0:T(8,128)(2,1)}, u32[]{:S(2)}) copy-start(bf16[320,320]{1,0:T(8,128)(2,1)} %param.20) | copy-start | bytes 614404
where the time goes:
time: 137 us; the launch traced here: 136 us
  local copies, waits for them, and re-layouts  42.6 us (31%)
  starting transfers between devices  41.5 us (30%)
  other arithmetic  24.7 us (18%)
  matrix products  21 us (15%)
  waiting for transfers between devices  5.39 us (4%)
    all_to_all x1, starting transfers between devices, summed_on_arrival(): lax.all_to_all(tiles, axis, split_axis=0, concat_axis=0, tiled=True)  14.6 us
    all_to_all x2, starting transfers between devices, copy_for_each(): return lax.all_to_all(copies, axis, split_axis=0, concat_axis=0, tiled=True)  11.8 us
    scatter-add x1, other arithmetic, body(): jax.ops.segment_sum(strength, host_element, num_segments=elements)  11.6 us
    ppermute x2, starting transfers between devices, extended(): lax.ppermute(lax.slice_in_dim(block, 0, width, axis=dim), axis, backward)  10.1 us
    unnamed x4, other arithmetic  9.23 us
    reshape x1, local copies, waits for them, and re-layouts, body(): stacked = jnp.concatenate([from_lower_axial, from_upper_axial, from_lower...  7.84 us
    reshape x1, local copies, waits for them, and re-layouts, body(): return (sens_own, updated.reshape(adjoint_state.shape))  7.55 us
    dot_general x1, matrix products, body(): jnp.dot(volume_operator, flat_state, preferred_element_type=jnp.float32)  6.64 us
  transfers between devices with their start and end apart: 7, of which 1 were waited for; matrix products, arithmetic and copies ran while one was open for 33% of the time, Pallas kernels for 0%

commit v1 on v0

v1 whole, which is shorter than its diff:
```python
import jax
import jax.numpy as jnp
import numpy as np
from jax import lax
from jax.experimental import pallas as pl
from jax.experimental.pallas import tpu as pltpu
from jax.sharding import PartitionSpec as P

MESH = pl.DeviceIdType.MESH
BF = jnp.bfloat16
F32 = jnp.float32
ANY = pl.BlockSpec(memory_space=pl.ANY)
VM = pl.BlockSpec(memory_space=pltpu.VMEM)
ROWS = 32
NT = (((1,), (1,)), ((), ()))
TN = (((0,), (0,)), ((), ()))


def dot(a, b, dims=(((1,), (0,)), ((), ()))):
    return lax.dot_general(a, b, dims, preferred_element_type=F32)


def halves(x):
    top = x.astype(BF)
    return top, (x - top.astype(F32)).astype(BF)


def peers_by_distance():
    def hops(d):
        return min(d, 4 - d)

    steps = [(dx, dy, dc) for dx in range(4) for dy in range(4) for dc in range(2)]
    steps = [s for s in steps if s != (0, 0, 0)]
    return sorted(steps, key=lambda s: -(hops(s[0]) + hops(s[1])))


def expander():
    e = np.zeros((480, 640), np.float32)
    for j in range(160):
        e[j, j] = 1.0
    for vp in range(20):
        for w in range(4):
            e[160 + vp * 4 + w, 160 + vp * 8 + 4 + w] = 1.0
            e[240 + vp * 4 + w, 320 + vp * 8 + w] = 1.0
    for j in range(160):
        e[320 + j, 480 + j] = 1.0
    return e


def kernel(
    sig_hbm, ret_hbm, rad_hbm, state_hbm, lift_hbm, vol_hbm, exp_hbm, target_hbm,
    taper_ref, wobs_ref, wsam_ref, host_ref,
    base_hbm, obs_ref, es_ref,
    sig, ret, rad, st, lift, vol, exp, target,
    d0, d1, g0, g1, part, recv_a, send_b, recv_b, sens, own_f, other_f,
    sf, rhs, lf, az_send, az_recv, oh_lo, tcol,
    ld, out_sem, sa, ra, sb, rb, sc, rc, sp, rp, hx_s, hx_r, ha_s, ha_r,
):
    s = lax.axis_index("stream")
    a = lax.axis_index("azim")
    core = s % 2
    z_lo = s // 2
    xy = a % 16
    z_hi = a // 16
    cx, cy = xy // 4, xy % 4
    q_me = core * 16 + xy
    z_me = z_hi * 4 + z_lo
    steps = peers_by_distance()

    def group_peer(step):
        dx, dy, dc = step
        return z_lo * 2 + (core + dc) % 2, z_hi * 16 + ((cx + dx) % 4) * 4 + (cy + dy) % 4

    def z_peer(dz):
        z = (z_me + dz) % 8
        return (z % 4) * 2 + core, (z // 4) * 16 + xy

    def q_of(peer):
        return (peer[0] % 2) * 16 + peer[1] % 16

    a_next, a_prev = (a + 1) % 32, (a + 31) % 32

    loads = {}

    def load(i, src, dst):
        loads[i] = pltpu.make_async_copy(src, dst, ld.at[i])
        loads[i].start()

    load(0, ret_hbm, ret)
    load(1, sig_hbm, sig)
    for c in range(4):
        load(2 + c, rad_hbm.at[pl.ds(c * 8, 8)], rad.at[pl.ds(c * 8, 8)])
    load(6, state_hbm, st)
    load(7, lift_hbm, lift)
    load(8, exp_hbm, exp)
    load(9, vol_hbm, vol)
    load(10, target_hbm, target)

    barrier = pltpu.get_barrier_semaphore()

    def greet(peer):
        pl.semaphore_signal(barrier, inc=1, device_id=peer, device_id_type=MESH)

    for step in steps:
        greet(group_peer(step))
    for dz in range(1, 8):
        greet(z_peer(dz))
    greet((s, a_next))
    greet((s, a_prev))

    @pl.when(s > 0)
    def _():
        greet((s - 1, a))

    @pl.when(s < 7)
    def _():
        greet((s + 1, a))

    loads[0].wait()
    loads[1].wait()
    d0[64:128, :] = jnp.zeros((64, 2048), BF)
    d1[0:64, :] = jnp.zeros((64, 2048), BF)
    for b in range(16):
        cols = slice(b * 128, b * 128 + 128)
        blk = dot(ret[b], sig[:, cols], TN).astype(BF)
        d0[0:64, cols] = blk
        d1[64:128, cols] = blk
    for c in range(4):
        loads[2 + c].wait()
    for g in range(2):
        q0 = g * 16
        acc = dot(rad[q0 : q0 + 16, 0].reshape(256, 2048), d0[...], NT)
        acc = acc + dot(rad[q0 : q0 + 16, 1].reshape(256, 2048), d1[...], NT)
        part[q0 : q0 + 16] = acc.reshape(16, 16, 128).astype(BF)

    extra = jnp.where(s > 0, 1, 0) + jnp.where(s < 7, 1, 0)
    pl.semaphore_wait(barrier, 40 + extra)

    for step in steps:
        peer = group_peer(step)
        pltpu.make_async_remote_copy(
            src_ref=part.at[q_of(peer)], dst_ref=recv_a.at[q_me], send_sem=sa, recv_sem=ra,
            device_id=peer, device_id_type=MESH,
        ).start()
    recv_a[q_me] = part[q_me]

    loads[6].wait()

    @pl.loop(0, 10)
    def _(i):
        sf[pl.ds(i * 1024, 1024), :] = st[pl.ds(i * 32, 32)].astype(F32).reshape(1024, 128)

    lane = lax.broadcasted_iota(jnp.int32, (80, 128), 1)

    @pl.loop(0, 4)
    def _(x):
        for ay in range(4):
            roll_up, roll_dn = [], []
            for rhi in range(2):
                r = x * 8 + rhi * 4 + ay
                col = pl.multiple_of((x * 8 + ay * 2 + rhi) * 128, 128)
                f = sf[pl.ds(r, 320, stride=ROWS), :]
                xb = f.astype(BF)
                rhs[640:960, pl.ds(col, 128)] = xb
                x5 = xb.reshape(5, 64, 128)

                @pl.when(x < 3)
                def _():
                    rhs[0:80, pl.ds(col + 1024, 128)] = x5[:, 48:64].reshape(80, 128)

                @pl.when(x > 0)
                def _():
                    rhs[80:160, pl.ds(col - 1024, 128)] = x5[:, 0:16].reshape(80, 128)

                tiles = f.reshape(20, 2, 8, 128)
                upper = tiles[:, 1]
                lower = tiles[:, 0]
                if ay < 3:
                    rhs[160:320, pl.ds(col + 256, 128)] = upper.reshape(160, 128).astype(BF)
                else:
                    u = upper.reshape(10, 2, 8, 128)
                    packed = jnp.concatenate([u[:, 0, 4:8], u[:, 1, 4:8]], axis=1)
                    az_send[0, :, pl.ds(pl.multiple_of(x * 256 + rhi * 128, 128), 128)] = packed.reshape(80, 128).astype(BF)
                if ay > 0:
                    rhs[320:480, pl.ds(col - 256, 128)] = lower.reshape(160, 128).astype(BF)
                else:
                    u = lower.reshape(10, 2, 8, 128)
                    packed = jnp.concatenate([u[:, 0, 0:4], u[:, 1, 0:4]], axis=1)
                    az_send[1, :, pl.ds(pl.multiple_of(x * 256 + rhi * 128, 128), 128)] = packed.reshape(80, 128).astype(BF)
                roll_up.append(pltpu.roll(sf[pl.ds(3 * ROWS + r, 80, stride=4 * ROWS), :], 1, 1))
                roll_dn.append(pltpu.roll(sf[pl.ds(r, 80, stride=4 * ROWS), :], 127, 1))
            col = pl.multiple_of((x * 8 + ay * 2) * 128, 128)
            zero = jnp.zeros((80, 128), F32)
            rhs[480:560, pl.ds(col, 128)] = jnp.where(lane == 0, zero, roll_up[0]).astype(BF)
            rhs[480:560, pl.ds(col + 128, 128)] = jnp.where(lane == 0, roll_up[0], roll_up[1]).astype(BF)
            rhs[560:640, pl.ds(col, 128)] = jnp.where(lane == 127, roll_dn[1], roll_dn[0]).astype(BF)
            rhs[560:640, pl.ds(col + 128, 128)] = jnp.where(lane == 127, zero, roll_dn[1]).astype(BF)

    az_up = pltpu.make_async_remote_copy(
        src_ref=az_send.at[0], dst_ref=az_recv.at[0], send_sem=ha_s.at[0], recv_sem=ha_r.at[0],
        device_id=(s, a_next), device_id_type=MESH)
    az_dn = pltpu.make_async_remote_copy(
        src_ref=az_send.at[1], dst_ref=az_recv.at[1], send_sem=ha_s.at[1], recv_sem=ha_r.at[1],
        device_id=(s, a_prev), device_id_type=MESH)
    az_up.start()
    az_dn.start()

    @pl.when(s < 7)
    def _():
        for v in range(5):
            pltpu.make_async_remote_copy(
                src_ref=rhs.at[pl.ds(640 + v * 64 + 48, 16), pl.ds(3072, 1024)],
                dst_ref=rhs.at[pl.ds(v * 16, 16), pl.ds(0, 1024)],
                send_sem=hx_s.at[0], recv_sem=hx_r.at[0],
                device_id=(s + 1, a), device_id_type=MESH).start()

    @pl.when(s > 0)
    def _():
        for v in range(5):
            pltpu.make_async_remote_copy(
                src_ref=rhs.at[pl.ds(640 + v * 64, 16), pl.ds(0, 1024)],
                dst_ref=rhs.at[pl.ds(80 + v * 16, 16), pl.ds(3072, 1024)],
                send_sem=hx_s.at[1], recv_sem=hx_r.at[1],
                device_id=(s - 1, a), device_id_type=MESH).start()

    @pl.when(s == 0)
    def _():
        rhs[0:80, 0:1024] = jnp.zeros((80, 1024), BF)

    @pl.when(s == 7)
    def _():
        rhs[80:160, 3072:4096] = jnp.zeros((80, 1024), BF)

    loads[10].wait()
    kb = pl.multiple_of((q_me // 4) * 128, 128)
    row = pl.multiple_of((q_me % 4) * 32, 32)

    def packed_columns(block):
        tcol[...] = jnp.transpose(block)
        return jnp.concatenate(
            [tcol[pl.ds(row, 16), :], tcol[pl.ds(pl.multiple_of(row + 16, 16), 16), :]], axis=1)

    target_own = packed_columns(target[:, pl.ds(kb, 128)])
    weight_own = packed_columns(taper_ref[...] * wobs_ref[:, pl.ds(kb, 128)])

    pltpu.make_async_copy(part.at[pl.ds(0, 31)], recv_a.at[pl.ds(0, 31)], ra).wait()
    send_b[...] = jnp.sum(recv_a[...].astype(F32), axis=0).astype(BF)
    for dz in (4, 3, 5, 2, 6, 1, 7):
        pltpu.make_async_remote_copy(
            src_ref=send_b, dst_ref=recv_b.at[z_me], send_sem=sb, recv_sem=rb,
            device_id=z_peer(dz), device_id_type=MESH,
        ).start()
    recv_b[z_me] = send_b[...]

    for i in (7, 8, 9):
        loads[i].wait()
    lf[:, 0:640] = dot(lift[...], exp[...]).astype(BF)
    lf[:, 640:960] = vol[...]

    def element_block(e):
        res = dot(lf[...], rhs[:, pl.ds(pl.multiple_of(e * 256, 256), 256)])
        x, ay = e // 4, e % 4
        for rhi in range(2):
            r = x * 8 + rhi * 4 + ay
            at = (pl.ds(r, 320, stride=ROWS), slice(None))
            sf[at] = sf[at] + res[:, rhi * 128 : rhi * 128 + 128]

    @pl.when(s > 0)
    def _():
        pltpu.make_async_copy(az_send.at[0], az_recv.at[0], hx_r.at[0]).wait()

    @pl.when(s < 7)
    def _():
        pltpu.make_async_copy(az_send.at[0], az_recv.at[0], hx_r.at[1]).wait()

    @pl.loop(0, 4)
    def _(x):
        element_block(x * 4 + 1)
        element_block(x * 4 + 2)

    pltpu.make_async_copy(part.at[pl.ds(0, 7)], recv_b.at[pl.ds(0, 7)], rb).wait()
    total = jnp.sum(recv_b[...].astype(F32), axis=0)
    own = weight_own * (total - target_own)
    own_f[...] = own
    sens[q_me] = own.astype(BF)
    for step in steps:
        pltpu.make_async_remote_copy(
            src_ref=sens.at[q_me], dst_ref=sens.at[q_me], send_sem=sc, recv_sem=rc,
            device_id=group_peer(step), device_id_type=MESH,
        ).start()
    swap = pltpu.make_async_remote_copy(
        src_ref=own_f, dst_ref=other_f, send_sem=sp, recv_sem=rp,
        device_id=((s + 1) - 2 * core, a), device_id_type=MESH)
    swap.start()

    w_hi, w_lo = halves(wsam_ref[...])
    w_lo2 = (wsam_ref[...] - w_hi.astype(F32) - w_lo.astype(F32)).astype(BF)
    w3 = jnp.concatenate([w_hi, w_lo, w_lo2], axis=0)
    g_rows = [jnp.sum(dot(w3, ret[b]), axis=0, keepdims=True) for b in range(16)]
    g_hi, g_lo = halves(jnp.concatenate(g_rows, axis=0))
    gg = jnp.concatenate([g_hi, g_lo], axis=0)
    blank = jnp.zeros((32, 64), BF)
    g0[...] = jnp.concatenate([gg, blank], axis=1)
    g1[...] = jnp.concatenate([blank, gg], axis=1)
    host = host_ref[...]
    lo = host % 128
    oh_lo[...] = jnp.where(lax.broadcasted_iota(jnp.int32, (128, 2048), 0) == lo, 1.0, 0.0).astype(BF)
    hi = host // 128
    point_row = (hi // 8) * 8 + (hi % 2) * 4 + (hi // 2) % 4

    az_up.wait()
    az_dn.wait()
    for x in range(4):
        for rhi in range(2):
            src = slice(x * 256 + rhi * 128, x * 256 + rhi * 128 + 128)
            up = az_recv[0, :, src].astype(F32).reshape(10, 8, 128)
            even = jnp.concatenate([up[:, 4:8], up[:, 0:4]], axis=1)
            both = jnp.concatenate([even[:, None], up[:, None]], axis=1)
            c0 = (x * 8 + rhi) * 128
            rhs[160:320, c0 : c0 + 128] = both.reshape(160, 128).astype(BF)
            dn = az_recv[1, :, src].astype(F32).reshape(10, 8, 128)
            odd = jnp.concatenate([dn[:, 4:8], dn[:, 0:4]], axis=1)
            both = jnp.concatenate([dn[:, None], odd[:, None]], axis=1)
            c3 = (x * 8 + 6 + rhi) * 128
            rhs[320:480, c3 : c3 + 128] = both.reshape(160, 128).astype(BF)

    @pl.loop(0, 4)
    def _(x):
        element_block(x * 4)
        element_block(x * 4 + 3)

    out = pltpu.make_async_copy(sf, base_hbm, out_sem)
    out.start()

    pltpu.make_async_copy(sens.at[pl.ds(0, 31)], sens.at[pl.ds(0, 31)], rc).wait()
    flat = sens[...].reshape(512, 128)
    h_low = []
    for g in (g0, g1):
        h = dot(g[...], flat, NT)
        h_low.append(jnp.concatenate(halves(h[0:16] + h[16:32]), axis=0))
    block_of = lax.broadcasted_iota(jnp.int32, (32, 512), 0) % 16
    es = jnp.zeros((64, 128), F32)
    for n in range(4):
        cols = slice(n * 512, n * 512 + 512)
        val = dot(h_low[0], rad[:, 0, :, cols].reshape(512, 512))
        val = val + dot(h_low[1], rad[:, 1, :, cols].reshape(512, 512))
        mine = lax.broadcasted_iota(jnp.int32, (32, 512), 1) // 128 + n * 4 == block_of
        strength = jnp.sum(jnp.where(mine, val, 0.0), axis=0, keepdims=True)
        rows = lax.broadcasted_iota(jnp.int32, (32, 512), 0)
        spread_rows = jnp.where(rows == point_row[:, cols], strength, 0.0)
        pieces = jnp.concatenate(halves(spread_rows), axis=0)
        es = es + dot(pieces, oh_lo[:, cols], NT)
    es_ref[...] = es[0:32] + es[32:64]

    swap.wait()
    mine_f = jnp.where(core == z_hi, own_f[...], other_f[...])
    obs_ref[0:16, :] = mine_f[:, 0:64]
    obs_ref[16:32, :] = mine_f[:, 64:128]

    pltpu.make_async_copy(part.at[pl.ds(0, 31)], recv_a.at[pl.ds(0, 31)], sa).wait()
    pltpu.make_async_copy(part.at[pl.ds(0, 7)], recv_b.at[pl.ds(0, 7)], sb).wait()
    pltpu.make_async_copy(sens.at[pl.ds(0, 31)], sens.at[pl.ds(0, 31)], sc).wait()

    @pl.when(s < 7)
    def _():
        pltpu.make_async_copy(az_send.at[0], az_recv.at[0], hx_s.at[0]).wait()

    @pl.when(s > 0)
    def _():
        pltpu.make_async_copy(az_send.at[0], az_recv.at[0], hx_s.at[1]).wait()

    out.wait()


def hann_taper(count):
    samples = np.arange(count, dtype=np.float32)
    return (0.5 - 0.5 * np.cos(2.0 * np.pi * (samples + 0.5) / count)).astype(np.float32)


def body(
    surface_signal, retarded_weights, radiation_weights, target_signal, observer_weights,
    sample_weights, host_element, source_profile, adjoint_state, volume_operator, lift_operator,
):
    dma = pltpu.SemaphoreType.DMA
    state = adjoint_state.reshape(320, 4, 4, 2, 128).transpose(0, 1, 3, 2, 4).reshape(320, 32, 128)
    taper = jnp.asarray(np.repeat(hann_taper(64)[:, None], 128, axis=1))
    expand = jnp.asarray(expander(), dtype=BF)
    base, obs_t, es = pl.pallas_call(
        kernel,
        out_shape=(
            jax.ShapeDtypeStruct((10240, 128), F32),
            jax.ShapeDtypeStruct((32, 64), F32),
            jax.ShapeDtypeStruct((32, 128), F32),
        ),
        in_specs=[ANY] * 8 + [VM] * 4,
        out_specs=(ANY, VM, VM),
        scratch_shapes=[
            pltpu.VMEM((64, 2048), BF),
            pltpu.VMEM((16, 64, 64), BF),
            pltpu.VMEM((32, 2, 16, 2048), BF),
            pltpu.VMEM((320, 32, 128), BF),
            pltpu.VMEM((320, 480), BF),
            pltpu.VMEM((320, 320), BF),
            pltpu.VMEM((480, 640), BF),
            pltpu.VMEM((64, 1024), F32),
            pltpu.VMEM((128, 2048), BF),
            pltpu.VMEM((128, 2048), BF),
            pltpu.VMEM((32, 128), BF),
            pltpu.VMEM((32, 128), BF),
            pltpu.VMEM((32, 16, 128), BF),
            pltpu.VMEM((32, 16, 128), BF),
            pltpu.VMEM((16, 128), BF),
            pltpu.VMEM((8, 16, 128), BF),
            pltpu.VMEM((32, 16, 128), BF),
            pltpu.VMEM((16, 128), F32),
            pltpu.VMEM((16, 128), F32),
            pltpu.VMEM((10240, 128), F32),
            pltpu.VMEM((960, 4096), BF),
            pltpu.VMEM((320, 960), BF),
            pltpu.VMEM((2, 80, 1024), BF),
            pltpu.VMEM((2, 80, 1024), BF),
            pltpu.VMEM((128, 2048), BF),
            pltpu.VMEM((128, 64), F32),
            dma((11,)),
            dma, dma, dma, dma, dma, dma, dma, dma, dma,
            dma((2,)), dma((2,)), dma((2,)), dma((2,)),
        ],
        compiler_params=pltpu.CompilerParams(
            collective_id=0, has_side_effects=True, vmem_limit_bytes=48 * 1024 * 1024
        ),
    )(
        surface_signal,
        retarded_weights,
        radiation_weights.reshape(32, 2, 16, 2048),
        state,
        lift_operator,
        volume_operator,
        expand,
        target_signal,
        taper,
        observer_weights.reshape(1, 1024),
        sample_weights.reshape(1, 64),
        host_element.reshape(1, 2048),
    )
    updated = base.reshape(320, 32, 128) + source_profile[:, None, None] * es[None]
    updated = updated.reshape(320, 4, 2, 4, 128).transpose(0, 1, 3, 2, 4)
    return (obs_t.T, updated.reshape(320, 4, 4, 256))


def solution(mesh):
    return jax.shard_map(
        body,
        mesh=mesh,
        in_specs=(
            P(None, ("stream", "azim")),
            P(("stream", "azim"), None, None),
            P(None, ("stream", "azim")),
            P(),
            P(),
            P(),
            P(("stream", "azim")),
            P(),
            P(None, "stream", "azim", None),
            P(),
            P(),
        ),
        out_specs=(P(None, "azim"), P(None, "stream", "azim", None)),
        check_vma=False,
    )
```

time: 137 us -> 66 us (0.48)
  Pallas kernels: 0 us -> 47.9 us
  starting transfers between devices: 41.5 us -> 0 us
  local copies, waits for them, and re-layouts: 42.6 us -> 11 us
  matrix products: 21 us -> 0 us
  other arithmetic: 24.7 us -> 5.87 us
  waiting for transfers between devices: 5.39 us -> 0 us
    pallas_call x0 -> x1, Pallas kernels: none -> 47.9 us  [body(): pl.pallas_call(kernel, out_shape=(jax.ShapeDtypeStruct((10240, 128), F32)...]
    all_to_all x3 -> x0, starting transfers between devices: 26.4 us -> none  [the longest x1 14.6 us: summed_on_arrival(): lax.all_to_all(tiles, axis, split_axis=0, concat_axis=0, tiled=True)]
    dot_general x6 -> x0, matrix products: 21 us -> none  [the longest x1 6.64 us: body(): jnp.dot(volume_operator, flat_state, preferred_element_type=jnp.float32)]
    reshape x4 -> x0, local copies, waits for them, and re-layouts: 19.7 us -> none  [the longest x1 7.84 us: body(): stacked = jnp.concatenate([from_lower_axial, from_upper_axial, from_lower...]
    ppermute x4 -> x0, starting transfers between devices: 15 us -> none  [the longest x2 10.1 us: extended(): lax.ppermute(lax.slice_in_dim(block, 0, width, axis=dim), axis, backward)]
    slice x11 -> x0, local copies, waits for them, and re-layouts: 13.7 us -> none  [the longest x1 2.31 us: body(): lower_sector[:, :, 1:]]
    scatter-add x1 -> x0, other arithmetic: 11.6 us -> none  [body(): jax.ops.segment_sum(strength, host_element, num_segments=elements)]
    unnamed x4 -> x0, other arithmetic: 9.23 us -> none
  transfers between devices with their start and end apart: 7 -> 0, of which waited for: 1 -> 0; matrix products, arithmetic and copies ran while one was open for 33% -> 0% of each run, Pallas kernels for 0% -> 0%
where the time goes in v1:
time: 66 us; the launch traced here: 65.5 us
  Pallas kernels  47.9 us (73%)
  local copies, waits for them, and re-layouts  11 us (17%)
  other arithmetic  5.87 us (9%)
  between operations  0.68 us (1%)
    pallas_call x1, Pallas kernels, body(): pl.pallas_call(kernel, out_shape=(jax.ShapeDtypeStruct((10240, 128), F32)...  47.9 us
    unnamed x25, local copies, waits for them, and re-layouts  11 us
    reshape x1, other arithmetic, body(): return (obs_t.T, updated.reshape(320, 4, 4, 256))  5.87 us

profile of v1, /device:TPU:1, one launch (start us, length us, event | category | flops | bytes accessed | tf_op | source)
XLA Modules:
  0.0 65.5 jit_solution(8540056720067895407)
XLA Ops:
  0.6 0.0 copy-start.11
  0.6 0.0 copy-start
  0.7 1.7 %copy-done = bf16[320,4,4,256]{3,2,1,0:T(4,128)(2,1)S(1)} copy-done((bf16[320,4,4,256]{3,2,1,0:T(4,128)(2,1)S(1)}, bf16[320,4,4,256]{3,2,1,0:T(4,128)(2,1)}, u32[]{:S(2)}) %copy-start) | copy-done | bytes 2621464
  2.4 0.0 copy-start.1
  2.4 1.1 %copy-done.1 = bf16[480,640]{1,0:T(8,128)(2,1)S(1)} copy-done((bf16[480,640]{1,0:T(8,128)(2,1)S(1)}, bf16[480,640]{1,0:T(8,128)(2,1)}, u32[]{:S(2)}) %copy-start.1) | copy-done | bytes 614424
  3.5 0.0 copy-start.2
  3.5 1.0 %copy-done.2 = bf16[320,480]{1,0:T(8,128)(2,1)S(1)} copy-done((bf16[320,480]{1,0:T(8,128)(2,1)S(1)}, bf16[320,480]{1,0:T(8,128)(2,1)}, u32[]{:S(2)}) %copy-start.2) | copy-done | bytes 307224
  4.4 0.0 copy-start.3
  4.4 0.9 %copy-done.3 = bf16[64,2048]{1,0:T(8,128)(2,1)S(1)} copy-done((bf16[64,2048]{1,0:T(8,128)(2,1)S(1)}, bf16[64,2048]{1,0:T(8,128)(2,1)}, u32[]{:S(2)}) %copy-start.3) | copy-done | bytes 262168
  5.4 0.0 copy-start.4
  5.4 0.9 %copy-done.4 = bf16[16,64,64]{2,1,0:T(8,128)(2,1)S(1)} copy-done((bf16[16,64,64]{2,1,0:T(8,128)(2,1)S(1)}, bf16[16,64,64]{2,1,0:T(8,128)(2,1)}, u32[]{:S(2)}) %copy-start.4) | copy-done | bytes 131096
  6.3 0.0 copy-start.5
  6.3 0.9 %copy-done.5 = f32[64,1024]{1,0:T(8,128)S(1)} copy-done((f32[64,1024]{1,0:T(8,128)S(1)}, f32[64,1024]{1,0:T(8,128)}, u32[]{:S(2)}) %copy-start.5) | copy-done | bytes 262168
  7.3 0.0 copy-start.6
  7.3 0.9 %copy-done.6 = bf16[320,320]{1,0:T(8,128)(2,1)S(1)} copy-done((bf16[320,320]{1,0:T(8,128)(2,1)S(1)}, bf16[320,320]{1,0:T(8,128)(2,1)}, u32[]{:S(2)}) %copy-start.6) | copy-done | bytes 204824
  8.2 0.8 %copy-done.7 = f32[64,128]{1,0:T(8,128)S(1)} copy-done((f32[64,128]{1,0:T(8,128)S(1)}, f32[64,128]{1,0:T(8,128)}, u32[]{:S(2)}) %copy-start.7) | copy-done | bytes 32792
  9.0 0.0 copy-start.8
  9.0 0.7 %copy-done.8 = s32[2048]{0:T(1024)S(1)} copy-done((s32[2048]{0:T(1024)S(1)}, s32[2048]{0:T(1024)}, u32[]{:S(2)}) %copy-start.8) | copy-done | bytes 8216
  9.7 0.7 %copy-done.9 = f32[1024]{0:T(1024)S(1)} copy-done((f32[1024]{0:T(1024)S(1)}, f32[1024]{0:T(1024)}, u32[]{:S(2)}) %copy-start.9) | copy-done | bytes 4120
  10.4 0.7 copy-done.10
  11.0 47.9 %shard_map.140 = (f32[10240,128]{1,0:T(8,128)}, f32[32,64]{1,0:T(8,128)S(1)}, f32[32,128]{1,0:T(8,128)S(1)}) custom-call(bf16[64,2048]{1,0:T(8,128)(2,1)S(1)} %copy-done.3, bf16[16,64,64]{2,1,0:T(8,128)(2,1)S(1)} %copy-done.4, bf16[32,2,16,2048]{3,2,1,0:T(8,128)(2,1)} %bitcast.23, bf16[320,32,128]{2,1,0:T(8,128)(2,1)S(1)} %bitcast.16, ...), custom_call_target="tpu_custom_call" | custom-call | tf_op jit(solution)/shard_map/pallas_call | solution.py:388
  59.0 0.0 copy-done.11
  59.0 5.9 %add_bitcast_fusion = f32[320,4,4,256]{3,2,1,0:T(4,128)} fusion(f32[320,4,2,4,128]{4,3,2,1,0:T(4,128)} %bitcast.22, f32[4,2,4,128]{3,2,1,0:T(4,128)S(1)} %bitcast.17, f32[320]{0:T(512)S(1)} %copy-done.11), kind=kLoop, calls=%fused_computation | loop fusion | flops 2621440 | bytes 10503424 | tf_op jit(solution)/shard_map/reshape | solution.py:447
  64.9 0.6 copy.18
  (3 shorter events, 0.0 us)
Async XLA Ops:
  0.6 58.3 %copy-start.11 = (f32[320]{0:T(512)S(1)}, f32[320]{0:T(512)}, u32[]{:S(2)}) copy-start(f32[320]{0:T(512)} %param.20) | copy-start | bytes 3844
  0.6 1.7 %copy-start = (bf16[320,4,4,256]{3,2,1,0:T(4,128)(2,1)S(1)}, bf16[320,4,4,256]{3,2,1,0:T(4,128)(2,1)}, u32[]{:S(2)}) copy-start(bf16[320,4,4,256]{3,2,1,0:T(4,128)(2,1)} %param.21) | copy-start | bytes 7864324
  2.4 1.1 %copy-start.1 = (bf16[480,640]{1,0:T(8,128)(2,1)S(1)}, bf16[480,640]{1,0:T(8,128)(2,1)}, u32[]{:S(2)}) copy-start(bf16[480,640]{1,0:T(8,128)(2,1)} %constant.5.clone.exp_hbm) | copy-start | bytes 1843204
  3.5 1.0 %copy-start.2 = (bf16[320,480]{1,0:T(8,128)(2,1)S(1)}, bf16[320,480]{1,0:T(8,128)(2,1)}, u32[]{:S(2)}) copy-start(bf16[320,480]{1,0:T(8,128)(2,1)} %lift_hbm.1) | copy-start | bytes 921604
  4.4 0.9 %copy-start.3 = (bf16[64,2048]{1,0:T(8,128)(2,1)S(1)}, bf16[64,2048]{1,0:T(8,128)(2,1)}, u32[]{:S(2)}) copy-start(bf16[64,2048]{1,0:T(8,128)(2,1)} %sig_hbm.1) | copy-start | bytes 786436
  5.4 0.9 %copy-start.4 = (bf16[16,64,64]{2,1,0:T(8,128)(2,1)S(1)}, bf16[16,64,64]{2,1,0:T(8,128)(2,1)}, u32[]{:S(2)}) copy-start(bf16[16,64,64]{2,1,0:T(8,128)(2,1)} %ret_hbm.1) | copy-start | bytes 393220
  6.3 0.9 %copy-start.5 = (f32[64,1024]{1,0:T(8,128)S(1)}, f32[64,1024]{1,0:T(8,128)}, u32[]{:S(2)}) copy-start(f32[64,1024]{1,0:T(8,128)} %target_hbm.1) | copy-start | bytes 786436
  7.3 0.9 %copy-start.6 = (bf16[320,320]{1,0:T(8,128)(2,1)S(1)}, bf16[320,320]{1,0:T(8,128)(2,1)}, u32[]{:S(2)}) copy-start(bf16[320,320]{1,0:T(8,128)(2,1)} %vol_hbm.1) | copy-start | bytes 614404
  8.2 0.8 %copy-start.7 = (f32[64,128]{1,0:T(8,128)S(1)}, f32[64,128]{1,0:T(8,128)}, u32[]{:S(2)}) copy-start(f32[64,128]{1,0:T(8,128)} %constant.4.clone.taper_ref) | copy-start | bytes 98308
  9.0 0.7 %copy-start.8 = (s32[2048]{0:T(1024)S(1)}, s32[2048]{0:T(1024)}, u32[]{:S(2)}) copy-start(s32[2048]{0:T(1024)} %param.19) | copy-start | bytes 24580
  9.7 0.7 %copy-start.9 = (f32[1024]{0:T(1024)S(1)}, f32[1024]{0:T(1024)}, u32[]{:S(2)}) copy-start(f32[1024]{0:T(1024)} %param.17) | copy-start | bytes 12292
  10.4 0.7 %copy-start.10 = (f32[64]{0:T(128)S(1)}, f32[64]{0:T(128)}, u32[]{:S(2)}) copy-start(f32[64]{0:T(128)} %param.18) | copy-start | bytes 772

commit v2 on v1

--- a/solution.py
+++ b/solution.py
@@ -11,7 +11,10 @@
 F32 = jnp.float32
 ANY = pl.BlockSpec(memory_space=pl.ANY)
 VM = pl.BlockSpec(memory_space=pltpu.VMEM)
+FINISH = 10
 ROWS = 32
+PITCH = 33
+FACE_PITCH = 9
 NT = (((1,), (1,)), ((), ()))
 TN = (((0,), (0,)), ((), ()))
 
@@ -49,12 +52,13 @@
 
 def kernel(
     sig_hbm, ret_hbm, rad_hbm, state_hbm, lift_hbm, vol_hbm, exp_hbm, target_hbm,
-    taper_ref, wobs_ref, wsam_ref, host_ref,
-    base_hbm, obs_ref, es_ref,
+    taper_hbm, wobs_hbm, wsam_hbm, host_hbm,
+    sf, obs_ref, es_ref,
     sig, ret, rad, st, lift, vol, exp, target,
     d0, d1, g0, g1, part, recv_a, send_b, recv_b, sens, own_f, other_f,
-    sf, rhs, lf, az_send, az_recv, oh_lo, tcol,
-    ld, out_sem, sa, ra, sb, rb, sc, rc, sp, rp, hx_s, hx_r, ha_s, ha_r,
+    rhs, lf, az_send, az_recv, ax_recv, axf, oh_lo, tcol,
+    taper_ref, wobs_ref, wsam_ref, host_ref,
+    ld, sa, ra, sb, rb, sc, rc, sp, rp, hx_s, hx_r, ha_s, ha_r,
 ):
     s = lax.axis_index("stream")
     a = lax.axis_index("azim")
@@ -66,6 +70,7 @@
     q_me = core * 16 + xy
     z_me = z_hi * 4 + z_lo
     steps = peers_by_distance()
+    planar = [(dx, dy) for dx, dy, dc in steps if dc == 1]
 
     def group_peer(step):
         dx, dy, dc = step
@@ -95,6 +100,10 @@
     load(8, exp_hbm, exp)
     load(9, vol_hbm, vol)
     load(10, target_hbm, target)
+    load(11, taper_hbm, taper_ref)
+    load(12, wobs_hbm, wobs_ref)
+    load(13, wsam_hbm, wsam_ref)
+    load(14, host_hbm, host_ref)
 
     barrier = pltpu.get_barrier_semaphore()
 
@@ -125,30 +134,60 @@
         blk = dot(ret[b], sig[:, cols], TN).astype(BF)
         d0[0:64, cols] = blk
         d1[64:128, cols] = blk
-    for c in range(4):
-        loads[2 + c].wait()
-    for g in range(2):
-        q0 = g * 16
-        acc = dot(rad[q0 : q0 + 16, 0].reshape(256, 2048), d0[...], NT)
-        acc = acc + dot(rad[q0 : q0 + 16, 1].reshape(256, 2048), d1[...], NT)
-        part[q0 : q0 + 16] = acc.reshape(16, 16, 128).astype(BF)
-
     extra = jnp.where(s > 0, 1, 0) + jnp.where(s < 7, 1, 0)
-    pl.semaphore_wait(barrier, 40 + extra)
-
-    for step in steps:
-        peer = group_peer(step)
+
+    def send_partial(peer):
         pltpu.make_async_remote_copy(
             src_ref=part.at[q_of(peer)], dst_ref=recv_a.at[q_me], send_sem=sa, recv_sem=ra,
             device_id=peer, device_id_type=MESH,
         ).start()
+
+    for g in range(2):
+        q0 = g * 16
+        loads[2 + 2 * g].wait()
+        loads[3 + 2 * g].wait()
+        acc = dot(rad[q0 : q0 + 16, 0].reshape(256, 2048), d0[...], NT)
+        acc = acc + dot(rad[q0 : q0 + 16, 1].reshape(256, 2048), d1[...], NT)
+        part[q0 : q0 + 16] = acc.reshape(16, 16, 128).astype(BF)
+        if g == 0:
+            pl.semaphore_wait(barrier, 40 + extra)
+        for dx, dy in planar:
+            peer = (z_lo * 2 + g, z_hi * 16 + ((cx + dx) % 4) * 4 + (cy + dy) % 4)
+            if (dx, dy) != (0, 0):
+                send_partial(peer)
+            else:
+
+                @pl.when(core != g)
+                def _():
+                    send_partial(peer)
+
+    @pl.when(s < 7)
+    def _():
+        for v in range(5):
+            pltpu.make_async_remote_copy(
+                src_ref=state_hbm.at[pl.ds(v * 64 + 48, 16), pl.ds(24, 8)],
+                dst_ref=ax_recv.at[0, pl.ds(v * 16, 16)],
+                send_sem=hx_s.at[0], recv_sem=hx_r.at[0],
+                device_id=(s + 1, a), device_id_type=MESH).start()
+
+    @pl.when(s > 0)
+    def _():
+        for v in range(5):
+            pltpu.make_async_remote_copy(
+                src_ref=state_hbm.at[pl.ds(v * 64, 16), pl.ds(0, 8)],
+                dst_ref=ax_recv.at[1, pl.ds(v * 16, 16)],
+                send_sem=hx_s.at[1], recv_sem=hx_r.at[1],
+                device_id=(s - 1, a), device_id_type=MESH).start()
+
     recv_a[q_me] = part[q_me]
 
     loads[6].wait()
 
-    @pl.loop(0, 10)
+    @pl.loop(0, 40)
     def _(i):
-        sf[pl.ds(i * 1024, 1024), :] = st[pl.ds(i * 32, 32)].astype(F32).reshape(1024, 128)
+        for j in range(8):
+            c = i * 8 + j
+            sf[pl.ds(c * PITCH, ROWS), :] = st[c].astype(F32)
 
     lane = lax.broadcasted_iota(jnp.int32, (80, 128), 1)
 
@@ -158,43 +197,43 @@
             roll_up, roll_dn = [], []
             for rhi in range(2):
                 r = x * 8 + rhi * 4 + ay
-                col = pl.multiple_of((x * 8 + ay * 2 + rhi) * 128, 128)
-                f = sf[pl.ds(r, 320, stride=ROWS), :]
+                col = pl.multiple_of(x * 256 + rhi * 128, 128)
+                f = sf[pl.ds(r, 320, stride=PITCH), :]
                 xb = f.astype(BF)
-                rhs[640:960, pl.ds(col, 128)] = xb
+                rhs[ay, 640:960, pl.ds(col, 128)] = xb
                 x5 = xb.reshape(5, 64, 128)
 
                 @pl.when(x < 3)
                 def _():
-                    rhs[0:80, pl.ds(col + 1024, 128)] = x5[:, 48:64].reshape(80, 128)
+                    rhs[ay, 0:80, pl.ds(col + 256, 128)] = x5[:, 48:64].reshape(80, 128)
 
                 @pl.when(x > 0)
                 def _():
-                    rhs[80:160, pl.ds(col - 1024, 128)] = x5[:, 0:16].reshape(80, 128)
+                    rhs[ay, 80:160, pl.ds(col - 256, 128)] = x5[:, 0:16].reshape(80, 128)
 
                 tiles = f.reshape(20, 2, 8, 128)
                 upper = tiles[:, 1]
                 lower = tiles[:, 0]
                 if ay < 3:
-                    rhs[160:320, pl.ds(col + 256, 128)] = upper.reshape(160, 128).astype(BF)
+                    rhs[ay + 1, 160:320, pl.ds(col, 128)] = upper.reshape(160, 128).astype(BF)
                 else:
                     u = upper.reshape(10, 2, 8, 128)
                     packed = jnp.concatenate([u[:, 0, 4:8], u[:, 1, 4:8]], axis=1)
-                    az_send[0, :, pl.ds(pl.multiple_of(x * 256 + rhi * 128, 128), 128)] = packed.reshape(80, 128).astype(BF)
+                    az_send[0, :, pl.ds(col, 128)] = packed.reshape(80, 128).astype(BF)
                 if ay > 0:
-                    rhs[320:480, pl.ds(col - 256, 128)] = lower.reshape(160, 128).astype(BF)
+                    rhs[ay - 1, 320:480, pl.ds(col, 128)] = lower.reshape(160, 128).astype(BF)
                 else:
                     u = lower.reshape(10, 2, 8, 128)
                     packed = jnp.concatenate([u[:, 0, 0:4], u[:, 1, 0:4]], axis=1)
-                    az_send[1, :, pl.ds(pl.multiple_of(x * 256 + rhi * 128, 128), 128)] = packed.reshape(80, 128).astype(BF)
-                roll_up.append(pltpu.roll(sf[pl.ds(3 * ROWS + r, 80, stride=4 * ROWS), :], 1, 1))
-                roll_dn.append(pltpu.roll(sf[pl.ds(r, 80, stride=4 * ROWS), :], 127, 1))
-            col = pl.multiple_of((x * 8 + ay * 2) * 128, 128)
+                    az_send[1, :, pl.ds(col, 128)] = packed.reshape(80, 128).astype(BF)
+                roll_up.append(pltpu.roll(sf[pl.ds(3 * PITCH + r, 80, stride=4 * PITCH), :], 1, 1))
+                roll_dn.append(pltpu.roll(sf[pl.ds(r, 80, stride=4 * PITCH), :], 127, 1))
+            col = pl.multiple_of(x * 256, 256)
             zero = jnp.zeros((80, 128), F32)
-            rhs[480:560, pl.ds(col, 128)] = jnp.where(lane == 0, zero, roll_up[0]).astype(BF)
-            rhs[480:560, pl.ds(col + 128, 128)] = jnp.where(lane == 0, roll_up[0], roll_up[1]).astype(BF)
-            rhs[560:640, pl.ds(col, 128)] = jnp.where(lane == 127, roll_dn[1], roll_dn[0]).astype(BF)
-            rhs[560:640, pl.ds(col + 128, 128)] = jnp.where(lane == 127, zero, roll_dn[1]).astype(BF)
+            rhs[ay, 480:560, pl.ds(col, 128)] = jnp.where(lane == 0, zero, roll_up[0]).astype(BF)
+            rhs[ay, 480:560, pl.ds(col + 128, 128)] = jnp.where(lane == 0, roll_up[0], roll_up[1]).astype(BF)
+            rhs[ay, 560:640, pl.ds(col, 128)] = jnp.where(lane == 127, roll_dn[1], roll_dn[0]).astype(BF)
+            rhs[ay, 560:640, pl.ds(col + 128, 128)] = jnp.where(lane == 127, zero, roll_dn[1]).astype(BF)
 
     az_up = pltpu.make_async_remote_copy(
         src_ref=az_send.at[0], dst_ref=az_recv.at[0], send_sem=ha_s.at[0], recv_sem=ha_r.at[0],
@@ -205,33 +244,16 @@
     az_up.start()
     az_dn.start()
 
-    @pl.when(s < 7)
-    def _():
-        for v in range(5):
-            pltpu.make_async_remote_copy(
-                src_ref=rhs.at[pl.ds(640 + v * 64 + 48, 16), pl.ds(3072, 1024)],
-                dst_ref=rhs.at[pl.ds(v * 16, 16), pl.ds(0, 1024)],
-                send_sem=hx_s.at[0], recv_sem=hx_r.at[0],
-                device_id=(s + 1, a), device_id_type=MESH).start()
-
-    @pl.when(s > 0)
-    def _():
-        for v in range(5):
-            pltpu.make_async_remote_copy(
-                src_ref=rhs.at[pl.ds(640 + v * 64, 16), pl.ds(0, 1024)],
-                dst_ref=rhs.at[pl.ds(80 + v * 16, 16), pl.ds(3072, 1024)],
-                send_sem=hx_s.at[1], recv_sem=hx_r.at[1],
-                device_id=(s - 1, a), device_id_type=MESH).start()
-
     @pl.when(s == 0)
     def _():
-        rhs[0:80, 0:1024] = jnp.zeros((80, 1024), BF)
+        rhs[:, 0:80, 0:256] = jnp.zeros((4, 80, 256), BF)
 
     @pl.when(s == 7)
     def _():
-        rhs[80:160, 3072:4096] = jnp.zeros((80, 1024), BF)
-
-    loads[10].wait()
+        rhs[:, 80:160, 768:1024] = jnp.zeros((4, 80, 256), BF)
+
+    for i in (10, 11, 12, 13, 14):
+        loads[i].wait()
     kb = pl.multiple_of((q_me // 4) * 128, 128)
     row = pl.multiple_of((q_me % 4) * 32, 32)
 
@@ -257,26 +279,34 @@
     lf[:, 0:640] = dot(lift[...], exp[...]).astype(BF)
     lf[:, 640:960] = vol[...]
 
-    def element_block(e):
-        res = dot(lf[...], rhs[:, pl.ds(pl.multiple_of(e * 256, 256), 256)])
-        x, ay = e // 4, e % 4
+    def sector_row(ay):
+        res = dot(lf[...], rhs[ay])
+        for x in range(4):
+            for rhi in range(2):
+                at = (pl.ds(x * 8 + rhi * 4 + ay, 320, stride=PITCH), slice(None))
+                col = x * 256 + rhi * 128
+                sf[at] = sf[at] + res[:, col : col + 128]
+
+    def axial_halo(side, row, col):
+        pltpu.make_async_copy(az_send.at[0], az_recv.at[0], hx_r.at[side]).wait()
+        for c in range(80):
+            axf[c * FACE_PITCH : c * FACE_PITCH + 8, :] = ax_recv[side, c].astype(F32)
         for rhi in range(2):
-            r = x * 8 + rhi * 4 + ay
-            at = (pl.ds(r, 320, stride=ROWS), slice(None))
-            sf[at] = sf[at] + res[:, rhi * 128 : rhi * 128 + 128]
+            for ay in range(4):
+                face = axf[pl.ds(rhi * 4 + ay, 80, stride=FACE_PITCH), :].astype(BF)
+                rhs[ay, row : row + 80, col + rhi * 128 : col + rhi * 128 + 128] = face
 
     @pl.when(s > 0)
     def _():
-        pltpu.make_async_copy(az_send.at[0], az_recv.at[0], hx_r.at[0]).wait()
+        axial_halo(0, 0, 0)
 
     @pl.when(s < 7)
     def _():
-        pltpu.make_async_copy(az_send.at[0], az_recv.at[0], hx_r.at[1]).wait()
-
-    @pl.loop(0, 4)
-    def _(x):
-        element_block(x * 4 + 1)
-        element_block(x * 4 + 2)
+        axial_halo(1, 80, 768)
+
+    @pl.loop(1, 3)
+    def _(ay):
+        sector_row(ay)
 
     pltpu.make_async_copy(part.at[pl.ds(0, 7)], recv_b.at[pl.ds(0, 7)], rb).wait()
     total = jnp.sum(recv_b[...].astype(F32), axis=0)
@@ -316,21 +346,15 @@
             up = az_recv[0, :, src].astype(F32).reshape(10, 8, 128)
             even = jnp.concatenate([up[:, 4:8], up[:, 0:4]], axis=1)
             both = jnp.concatenate([even[:, None], up[:, None]], axis=1)
-            c0 = (x * 8 + rhi) * 128
-            rhs[160:320, c0 : c0 + 128] = both.reshape(160, 128).astype(BF)
+            rhs[0, 160:320, src] = both.reshape(160, 128).astype(BF)
             dn = az_recv[1, :, src].astype(F32).reshape(10, 8, 128)
             odd = jnp.concatenate([dn[:, 4:8], dn[:, 0:4]], axis=1)
             both = jnp.concatenate([dn[:, None], odd[:, None]], axis=1)
-            c3 = (x * 8 + 6 + rhi) * 128
-            rhs[320:480, c3 : c3 + 128] = both.reshape(160, 128).astype(BF)
-
-    @pl.loop(0, 4)
-    def _(x):
-        element_block(x * 4)
-        element_block(x * 4 + 3)
-
-    out = pltpu.make_async_copy(sf, base_hbm, out_sem)
-    out.start()
+            rhs[3, 320:480, src] = both.reshape(160, 128).astype(BF)
+
+    @pl.loop(0, 2)
+    def _(i):
+        sector_row(i * 3)
 
     pltpu.make_async_copy(sens.at[pl.ds(0, 31)], sens.at[pl.ds(0, 31)], rc).wait()
     flat = sens[...].reshape(512, 128)
@@ -369,7 +393,26 @@
     def _():
         pltpu.make_async_copy(az_send.at[0], az_recv.at[0], hx_s.at[1]).wait()
 
-    out.wait()
+
+def finish(base_ref, es_ref, prof_ref, obs_in, out_hbm, obs_out, buf, sems):
+    obs_out[...] = obs_in[...]
+    es = es_ref[...]
+    copies = []
+    for k in range(FINISH):
+        n = 320 // FINISH
+
+        @pl.loop(0, n // 8)
+        def _(i):
+            for j in range(8):
+                c = k * n + i * 8 + j
+                rows = pl.ds(pl.multiple_of(c * ROWS, ROWS), ROWS)
+                buf[rows, :] = base_ref[pl.ds(c * PITCH, ROWS), :] + prof_ref[c] * es
+
+        part = pl.ds(k * n * ROWS, n * ROWS)
+        copies.append(pltpu.make_async_copy(buf.at[part], out_hbm.at[part], sems.at[k]))
+        copies[-1].start()
+    for c in copies:
+        c.wait()
 
 
 def hann_taper(count):
@@ -388,12 +431,12 @@
     base, obs_t, es = pl.pallas_call(
         kernel,
         out_shape=(
-            jax.ShapeDtypeStruct((10240, 128), F32),
+            pltpu.VMEM((320 * PITCH, 128), F32),
             jax.ShapeDtypeStruct((32, 64), F32),
             jax.ShapeDtypeStruct((32, 128), F32),
         ),
-        in_specs=[ANY] * 8 + [VM] * 4,
-        out_specs=(ANY, VM, VM),
+        in_specs=[ANY] * 12,
+        out_specs=(VM, VM, VM),
         scratch_shapes=[
             pltpu.VMEM((64, 2048), BF),
             pltpu.VMEM((16, 64, 64), BF),
@@ -414,35 +457,55 @@
             pltpu.VMEM((32, 16, 128), BF),
             pltpu.VMEM((16, 128), F32),
             pltpu.VMEM((16, 128), F32),
-            pltpu.VMEM((10240, 128), F32),
-            pltpu.VMEM((960, 4096), BF),
+            pltpu.VMEM((4, 960, 1024), BF),
             pltpu.VMEM((320, 960), BF),
             pltpu.VMEM((2, 80, 1024), BF),
             pltpu.VMEM((2, 80, 1024), BF),
+            pltpu.VMEM((2, 80, 8, 128), BF),
+            pltpu.VMEM((80 * FACE_PITCH, 128), F32),
             pltpu.VMEM((128, 2048), BF),
             pltpu.VMEM((128, 64), F32),
-            dma((11,)),
-            dma, dma, dma, dma, dma, dma, dma, dma, dma,
+            pltpu.VMEM((64, 128), F32),
+            pltpu.VMEM((1, 1024), F32),
+            pltpu.VMEM((1, 64), F32),
+            pltpu.VMEM((1, 2048), jnp.int32),
+            dma((15,)),
+            dma, dma, dma, dma, dma, dma, dma, dma,
             dma((2,)), dma((2,)), dma((2,)), dma((2,)),
         ],
         compiler_params=pltpu.CompilerParams(
             collective_id=0, has_side_effects=True, vmem_limit_bytes=48 * 1024 * 1024
         ),
     )(
-        surface_signal,
-        retarded_weights,
-        radiation_weights.reshape(32, 2, 16, 2048),
-        state,
-        lift_operator,
-        volume_operator,
-        expand,
-        target_signal,
-        taper,
-        observer_weights.reshape(1, 1024),
-        sample_weights.reshape(1, 64),
-        host_element.reshape(1, 2048),
+        *(
+            pltpu.with_memory_space_constraint(x, pltpu.HBM)
+            for x in (
+                surface_signal,
+                retarded_weights,
+                radiation_weights.reshape(32, 2, 16, 2048),
+                state,
+                lift_operator,
+                volume_operator,
+                expand,
+                target_signal,
+                taper,
+                observer_weights.reshape(1, 1024),
+                sample_weights.reshape(1, 64),
+                host_element.reshape(1, 2048),
+            )
+        )
     )
-    updated = base.reshape(320, 32, 128) + source_profile[:, None, None] * es[None]
+    updated, obs_t = pl.pallas_call(
+        finish,
+        out_shape=(
+            jax.ShapeDtypeStruct((10240, 128), F32),
+            jax.ShapeDtypeStruct((32, 64), F32),
+        ),
+        in_specs=[VM, VM, pl.BlockSpec(memory_space=pltpu.SMEM), VM],
+        out_specs=(ANY, VM),
+        scratch_shapes=[pltpu.VMEM((10240, 128), F32), dma((FINISH,))],
+        compiler_params=pltpu.CompilerParams(vmem_limit_bytes=16 * 1024 * 1024),
+    )(pltpu.with_memory_space_constraint(base, pltpu.VMEM), es, source_profile, obs_t)
     updated = updated.reshape(320, 4, 2, 4, 128).transpose(0, 1, 3, 2, 4)
     return (obs_t.T, updated.reshape(320, 4, 4, 256))
 

time: 66 us -> 37.8 us (0.57)
  local copies, waits for them, and re-layouts: 11 us -> 0.01 us
  Pallas kernels: 47.9 us -> 37 us
  other arithmetic: 5.87 us -> 0 us
    unnamed x25 -> x2, local copies, waits for them, and re-layouts: 11 us -> 0.01 us
    pallas_call x1 -> x2, Pallas kernels: 47.9 us -> 37 us  [the longest x1 33.4 us: body(): pl.pallas_call(kernel, out_shape=(pltpu.VMEM((320 * PITCH, 128), F32), ja...]
    reshape x1 -> x0, other arithmetic: 5.87 us -> none  [body(): return (obs_t.T, updated.reshape(320, 4, 4, 256))]
where the time goes in v2:
time: 37.8 us; the launch traced here: 37.7 us
  Pallas kernels  37 us (98%)
  between operations  0.66 us (2%)
    pallas_call x1, Pallas kernels, body(): pl.pallas_call(kernel, out_shape=(pltpu.VMEM((320 * PITCH, 128), F32), ja...  33.4 us
    pallas_call x1, Pallas kernels, body(): pl.pallas_call(finish, out_shape=(jax.ShapeDtypeStruct((10240, 128), F32)...  3.65 us

profile of v2, /device:TPU:1, one launch (start us, length us, event | category | flops | bytes accessed | tf_op | source)
XLA Modules:
  0.0 37.7 jit_solution(13384515407383314883)
XLA Ops:
  0.6 0.0 copy-start
  0.6 33.4 %shard_map.140 = (f32[10560,128]{1,0:T(8,128)S(1)}, f32[32,64]{1,0:T(8,128)S(1)}, f32[32,128]{1,0:T(8,128)S(1)}) custom-call(bf16[64,2048]{1,0:T(8,128)(2,1)} %sig_hbm.1, bf16[16,64,64]{2,1,0:T(8,128)(2,1)} %ret_hbm.1, bf16[32,2,16,2048]{3,2,1,0:T(8,128)(2,1)} %bitcast.15, bf16[320,32,128]{2,1,0:T(8,128)(2,1)} %bitcast.16, bf16[320,480]{1,0:T(8,128)(2,1)} %lift_hbm.1, ...), custom_call_target="tpu_custom_call" | custom-call | tf_op jit(solution)/shard_map/pallas_call | solution.py:431
  34.0 0.0 copy-done
  34.0 3.6 %shard_map.141 = (f32[10240,128]{1,0:T(8,128)}, f32[32,64]{1,0:T(8,128)}) custom-call(f32[10560,128]{1,0:T(8,128)S(1)} %get-tuple-element.7.base_ref, f32[32,128]{1,0:T(8,128)S(1)} %get-tuple-element.8.es_ref, f32[320]{0:T(512)S(1)} %copy-done, f32[32,64]{1,0:T(8,128)S(1)} %get-tuple-element.9.obs_in), custom_call_target="tpu_custom_call" | custom-call | tf_op jit(solution)/shard_map/pallas_call | solution.py:498
Async XLA Ops:
  0.6 33.4 %copy-start = (f32[320]{0:T(512)S(1)}, f32[320]{0:T(512)}, u32[]{:S(2)}) copy-start(f32[320]{0:T(512)} %prof_ref.1) | copy-start | bytes 3844

commit v3 on v2

--- a/solution.py
+++ b/solution.py
@@ -15,6 +15,7 @@
 ROWS = 32
 PITCH = 33
 FACE_PITCH = 9
+RELAYS = ((12, 3, 14, 11), (1, 4, 13, 7))
 NT = (((1,), (1,)), ((), ()))
 TN = (((0,), (0,)), ((), ()))
 
@@ -52,13 +53,13 @@
 
 def kernel(
     sig_hbm, ret_hbm, rad_hbm, state_hbm, lift_hbm, vol_hbm, exp_hbm, target_hbm,
-    taper_hbm, wobs_hbm, wsam_hbm, host_hbm,
-    sf, obs_ref, es_ref,
+    taper_hbm, wobs_hbm, wsam_hbm, host_hbm, prof_hbm,
+    sf, obs_ref, es_ref, prof_rows,
     sig, ret, rad, st, lift, vol, exp, target,
     d0, d1, g0, g1, part, recv_a, send_b, recv_b, sens, own_f, other_f,
     rhs, lf, az_send, az_recv, ax_recv, axf, oh_lo, tcol,
-    taper_ref, wobs_ref, wsam_ref, host_ref,
-    ld, sa, ra, sb, rb, sc, rc, sp, rp, hx_s, hx_r, ha_s, ha_r,
+    taper_ref, wobs_ref, wsam_ref, host_ref, prof_ref, relay,
+    ld, sa, ra, sb, rb, sc, rc, sp, rp, hx_s, hx_r, ha_s, ha_r, rel_s, rel_r,
 ):
     s = lax.axis_index("stream")
     a = lax.axis_index("azim")
@@ -70,7 +71,6 @@
     q_me = core * 16 + xy
     z_me = z_hi * 4 + z_lo
     steps = peers_by_distance()
-    planar = [(dx, dy) for dx, dy, dc in steps if dc == 1]
 
     def group_peer(step):
         dx, dy, dc = step
@@ -95,15 +95,18 @@
     load(1, sig_hbm, sig)
     for c in range(4):
         load(2 + c, rad_hbm.at[pl.ds(c * 8, 8)], rad.at[pl.ds(c * 8, 8)])
-    load(6, state_hbm, st)
-    load(7, lift_hbm, lift)
-    load(8, exp_hbm, exp)
-    load(9, vol_hbm, vol)
-    load(10, target_hbm, target)
-    load(11, taper_hbm, taper_ref)
-    load(12, wobs_hbm, wobs_ref)
-    load(13, wsam_hbm, wsam_ref)
-    load(14, host_hbm, host_ref)
+
+    def load_rest():
+        load(6, state_hbm, st)
+        load(7, lift_hbm, lift)
+        load(8, exp_hbm, exp)
+        load(9, vol_hbm, vol)
+        load(10, target_hbm, target)
+        load(11, taper_hbm, taper_ref)
+        load(12, wobs_hbm, wobs_ref)
+        load(13, wsam_hbm, wsam_ref)
+        load(14, host_hbm, host_ref)
+        load(15, prof_hbm, prof_ref)
 
     barrier = pltpu.get_barrier_semaphore()
 
@@ -124,6 +127,14 @@
     @pl.when(s < 7)
     def _():
         greet((s + 1, a))
+
+    ends = (15, 0)
+    for way in range(2):
+        for k in RELAYS[way]:
+
+            @pl.when(xy == ends[1 - way])
+            def _():
+                greet((s, (1 - z_hi) * 16 + k))
 
     loads[0].wait()
     loads[1].wait()
@@ -135,6 +146,8 @@
         d0[0:64, cols] = blk
         d1[64:128, cols] = blk
     extra = jnp.where(s > 0, 1, 0) + jnp.where(s < 7, 1, 0)
+    for k in RELAYS[0] + RELAYS[1]:
+        extra = extra + jnp.where(xy == k, 1, 0)
 
     def send_partial(peer):
         pltpu.make_async_remote_copy(
@@ -142,24 +155,27 @@
             device_id=peer, device_id_type=MESH,
         ).start()
 
-    for g in range(2):
-        q0 = g * 16
-        loads[2 + 2 * g].wait()
-        loads[3 + 2 * g].wait()
-        acc = dot(rad[q0 : q0 + 16, 0].reshape(256, 2048), d0[...], NT)
-        acc = acc + dot(rad[q0 : q0 + 16, 1].reshape(256, 2048), d1[...], NT)
-        part[q0 : q0 + 16] = acc.reshape(16, 16, 128).astype(BF)
+    for g in range(4):
+        q0 = g * 8
+        loads[2 + g].wait()
+        acc = dot(rad[q0 : q0 + 8, 0].reshape(128, 2048), d0[...], NT)
+        acc = acc + dot(rad[q0 : q0 + 8, 1].reshape(128, 2048), d1[...], NT)
+        part[q0 : q0 + 8] = acc.reshape(8, 16, 128).astype(BF)
         if g == 0:
             pl.semaphore_wait(barrier, 40 + extra)
-        for dx, dy in planar:
-            peer = (z_lo * 2 + g, z_hi * 16 + ((cx + dx) % 4) * 4 + (cy + dy) % 4)
-            if (dx, dy) != (0, 0):
-                send_partial(peer)
-            else:
-
-                @pl.when(core != g)
-                def _():
+        if g == 2:
+            load_rest()
+        for dx in (1, 0):
+            for dy in (2, 1, 3, 0):
+                px, py = (g % 2) * 2 + (cx + dx) % 2, (cy + dy) % 4
+                peer = (z_lo * 2 + g // 2, z_hi * 16 + px * 4 + py)
+                if dy != 0:
                     send_partial(peer)
+                else:
+
+                    @pl.when(q_of(peer) != q_me)
+                    def _():
+                        send_partial(peer)
 
     @pl.when(s < 7)
     def _():
@@ -188,6 +204,38 @@
         for j in range(8):
             c = i * 8 + j
             sf[pl.ds(c * PITCH, ROWS), :] = st[c].astype(F32)
+
+    @pl.loop(0, 4)
+    def _(x):
+        for rhi in range(2):
+            col = pl.multiple_of(x * 256 + rhi * 128, 128)
+            last = sf[pl.ds(x * 8 + rhi * 4 + 3, 320, stride=PITCH), :].reshape(10, 2, 2, 8, 128)
+            packed = jnp.concatenate([last[:, 0, 1, 4:8], last[:, 1, 1, 4:8]], axis=1)
+            az_send[0, :, pl.ds(col, 128)] = packed.reshape(80, 128).astype(BF)
+            first = sf[pl.ds(x * 8 + rhi * 4, 320, stride=PITCH), :].reshape(10, 2, 2, 8, 128)
+            packed = jnp.concatenate([first[:, 0, 0, 0:4], first[:, 1, 0, 0:4]], axis=1)
+            az_send[1, :, pl.ds(col, 128)] = packed.reshape(80, 128).astype(BF)
+
+    def az_copy(way, dst):
+        return pltpu.make_async_remote_copy(
+            src_ref=az_send.at[way], dst_ref=az_recv.at[way], send_sem=ha_s.at[way],
+            recv_sem=ha_r.at[way], device_id=(s, dst), device_id_type=MESH)
+
+    az_up, az_dn = az_copy(0, a_next), az_copy(1, a_prev)
+    for way, dst in ((0, a_next), (1, a_prev)):
+
+        @pl.when(xy == ends[way])
+        def _():
+            for i, k in enumerate(RELAYS[way]):
+                pltpu.make_async_remote_copy(
+                    src_ref=az_send.at[way, pl.ds(16 * i + 16, 16)], dst_ref=relay,
+                    send_sem=ha_s.at[way], recv_sem=rel_r,
+                    device_id=(s, z_hi * 16 + k), device_id_type=MESH).start()
+            first = pl.ds(0, 16)
+            pltpu.make_async_remote_copy(
+                src_ref=az_send.at[way, first], dst_ref=az_recv.at[way, first],
+                send_sem=ha_s.at[way], recv_sem=ha_r.at[way],
+                device_id=(s, dst), device_id_type=MESH).start()
 
     lane = lax.broadcasted_iota(jnp.int32, (80, 128), 1)
 
@@ -216,16 +264,8 @@
                 lower = tiles[:, 0]
                 if ay < 3:
                     rhs[ay + 1, 160:320, pl.ds(col, 128)] = upper.reshape(160, 128).astype(BF)
-                else:
-                    u = upper.reshape(10, 2, 8, 128)
-                    packed = jnp.concatenate([u[:, 0, 4:8], u[:, 1, 4:8]], axis=1)
-                    az_send[0, :, pl.ds(col, 128)] = packed.reshape(80, 128).astype(BF)
                 if ay > 0:
                     rhs[ay - 1, 320:480, pl.ds(col, 128)] = lower.reshape(160, 128).astype(BF)
-                else:
-                    u = lower.reshape(10, 2, 8, 128)
-                    packed = jnp.concatenate([u[:, 0, 0:4], u[:, 1, 0:4]], axis=1)
-                    az_send[1, :, pl.ds(col, 128)] = packed.reshape(80, 128).astype(BF)
                 roll_up.append(pltpu.roll(sf[pl.ds(3 * PITCH + r, 80, stride=4 * PITCH), :], 1, 1))
                 roll_dn.append(pltpu.roll(sf[pl.ds(r, 80, stride=4 * PITCH), :], 127, 1))
             col = pl.multiple_of(x * 256, 256)
@@ -235,14 +275,13 @@
             rhs[ay, 560:640, pl.ds(col, 128)] = jnp.where(lane == 127, roll_dn[1], roll_dn[0]).astype(BF)
             rhs[ay, 560:640, pl.ds(col + 128, 128)] = jnp.where(lane == 127, zero, roll_dn[1]).astype(BF)
 
-    az_up = pltpu.make_async_remote_copy(
-        src_ref=az_send.at[0], dst_ref=az_recv.at[0], send_sem=ha_s.at[0], recv_sem=ha_r.at[0],
-        device_id=(s, a_next), device_id_type=MESH)
-    az_dn = pltpu.make_async_remote_copy(
-        src_ref=az_send.at[1], dst_ref=az_recv.at[1], send_sem=ha_s.at[1], recv_sem=ha_r.at[1],
-        device_id=(s, a_prev), device_id_type=MESH)
-    az_up.start()
-    az_dn.start()
+    @pl.when(xy < 15)
+    def _():
+        az_up.start()
+
+    @pl.when(xy > 0)
+    def _():
+        az_dn.start()
 
     @pl.when(s == 0)
     def _():
@@ -252,8 +291,11 @@
     def _():
         rhs[:, 80:160, 768:1024] = jnp.zeros((4, 80, 256), BF)
 
-    for i in (10, 11, 12, 13, 14):
+    for i in (10, 11, 12, 13, 14, 15):
         loads[i].wait()
+    for c0, c1 in ((0, 128), (128, 256), (256, 320)):
+        line = prof_ref[c0:c1].reshape(1, c1 - c0)
+        prof_rows[c0:c1, :] = jnp.transpose(jnp.broadcast_to(line, (128, c1 - c0)))
     kb = pl.multiple_of((q_me // 4) * 128, 128)
     row = pl.multiple_of((q_me % 4) * 32, 32)
 
@@ -273,6 +315,20 @@
             device_id=z_peer(dz), device_id_type=MESH,
         ).start()
     recv_b[z_me] = send_b[...]
+
+    def forward(way):
+        for i, k in enumerate(RELAYS[way]):
+
+            @pl.when(xy == k)
+            def _():
+                pltpu.make_async_copy(az_send.at[0, pl.ds(0, 16)], relay, rel_r).wait()
+                rows = pl.ds(16 * i + 16, 16)
+                pltpu.make_async_remote_copy(
+                    src_ref=relay, dst_ref=az_recv.at[way, rows], send_sem=rel_s, recv_sem=ha_r.at[way],
+                    device_id=(s, (1 - z_hi) * 16 + ends[1 - way]), device_id_type=MESH).start()
+
+    forward(0)
+    forward(1)
 
     for i in (7, 8, 9):
         loads[i].wait()
@@ -393,11 +449,17 @@
     def _():
         pltpu.make_async_copy(az_send.at[0], az_recv.at[0], hx_s.at[1]).wait()
 
+    for k in RELAYS[0] + RELAYS[1]:
+
+        @pl.when(xy == k)
+        def _():
+            pltpu.make_async_copy(az_send.at[0, pl.ds(0, 16)], relay, rel_s).wait()
+
 
 def finish(base_ref, es_ref, prof_ref, obs_in, out_hbm, obs_out, buf, sems):
-    obs_out[...] = obs_in[...]
+    copies = [pltpu.make_async_copy(obs_in, obs_out, sems.at[FINISH])]
+    copies[0].start()
     es = es_ref[...]
-    copies = []
     for k in range(FINISH):
         n = 320 // FINISH
 
@@ -406,7 +468,7 @@
             for j in range(8):
                 c = k * n + i * 8 + j
                 rows = pl.ds(pl.multiple_of(c * ROWS, ROWS), ROWS)
-                buf[rows, :] = base_ref[pl.ds(c * PITCH, ROWS), :] + prof_ref[c] * es
+                buf[rows, :] = base_ref[pl.ds(c * PITCH, ROWS), :] + prof_ref[pl.ds(c, 1), :] * es
 
         part = pl.ds(k * n * ROWS, n * ROWS)
         copies.append(pltpu.make_async_copy(buf.at[part], out_hbm.at[part], sems.at[k]))
@@ -428,15 +490,16 @@
     state = adjoint_state.reshape(320, 4, 4, 2, 128).transpose(0, 1, 3, 2, 4).reshape(320, 32, 128)
     taper = jnp.asarray(np.repeat(hann_taper(64)[:, None], 128, axis=1))
     expand = jnp.asarray(expander(), dtype=BF)
-    base, obs_t, es = pl.pallas_call(
+    base, obs_t, es, prof_rows = pl.pallas_call(
         kernel,
         out_shape=(
             pltpu.VMEM((320 * PITCH, 128), F32),
             jax.ShapeDtypeStruct((32, 64), F32),
             jax.ShapeDtypeStruct((32, 128), F32),
+            pltpu.VMEM((320, 128), F32),
         ),
-        in_specs=[ANY] * 12,
-        out_specs=(VM, VM, VM),
+        in_specs=[ANY] * 13,
+        out_specs=(VM, VM, VM, VM),
         scratch_shapes=[
             pltpu.VMEM((64, 2048), BF),
             pltpu.VMEM((16, 64, 64), BF),
@@ -469,9 +532,11 @@
             pltpu.VMEM((1, 1024), F32),
             pltpu.VMEM((1, 64), F32),
             pltpu.VMEM((1, 2048), jnp.int32),
-            dma((15,)),
+            pltpu.VMEM((320,), F32),
+            pltpu.VMEM((16, 1024), BF),
+            dma((16,)),
             dma, dma, dma, dma, dma, dma, dma, dma,
-            dma((2,)), dma((2,)), dma((2,)), dma((2,)),
+            dma((2,)), dma((2,)), dma((2,)), dma((2,)), dma, dma,
         ],
         compiler_params=pltpu.CompilerParams(
             collective_id=0, has_side_effects=True, vmem_limit_bytes=48 * 1024 * 1024
@@ -492,6 +557,7 @@
                 observer_weights.reshape(1, 1024),
                 sample_weights.reshape(1, 64),
                 host_element.reshape(1, 2048),
+                source_profile,
             )
         )
     )
@@ -501,11 +567,16 @@
             jax.ShapeDtypeStruct((10240, 128), F32),
             jax.ShapeDtypeStruct((32, 64), F32),
         ),
-        in_specs=[VM, VM, pl.BlockSpec(memory_space=pltpu.SMEM), VM],
-        out_specs=(ANY, VM),
-        scratch_shapes=[pltpu.VMEM((10240, 128), F32), dma((FINISH,))],
+        in_specs=[VM, VM, VM, VM],
+        out_specs=(ANY, ANY),
+        scratch_shapes=[pltpu.VMEM((10240, 128), F32), dma((FINISH + 1,))],
         compiler_params=pltpu.CompilerParams(vmem_limit_bytes=16 * 1024 * 1024),
-    )(pltpu.with_memory_space_constraint(base, pltpu.VMEM), es, source_profile, obs_t)
+    )(
+        pltpu.with_memory_space_constraint(base, pltpu.VMEM),
+        es,
+        pltpu.with_memory_space_constraint(prof_rows, pltpu.VMEM),
+        obs_t,
+    )
     updated = updated.reshape(320, 4, 2, 4, 128).transpose(0, 1, 3, 2, 4)
     return (obs_t.T, updated.reshape(320, 4, 4, 256))
 

time: 37.8 us -> 33.1 us (0.88)
  Pallas kernels: 37 us -> 32.4 us
    pallas_call x1, Pallas kernels: 33.4 us -> 29.9 us  [body(): pl.pallas_call(kernel, out_shape=(pltpu.VMEM((320 * PITCH, 128), F32), ja...]
    pallas_call x1, Pallas kernels: 3.65 us -> 2.48 us  [body(): pl.pallas_call(finish, out_shape=(jax.ShapeDtypeStruct((10240, 128), F32)...]
where the time goes in v3:
time: 33.1 us
  Pallas kernels  32.4 us (98%)
  between operations  0.64 us (2%)
    pallas_call x1, Pallas kernels, body(): pl.pallas_call(kernel, out_shape=(pltpu.VMEM((320 * PITCH, 128), F32), ja...  29.9 us
    pallas_call x1, Pallas kernels, body(): pl.pallas_call(finish, out_shape=(jax.ShapeDtypeStruct((10240, 128), F32)...  2.48 us

profile of v3, /device:TPU:1, one launch (start us, length us, event | category | flops | bytes accessed | tf_op | source)
XLA Modules:
  0.0 33.1 jit_solution(16190427444701308743)
XLA Ops:
  0.6 29.9 %shard_map.140 = (f32[10560,128]{1,0:T(8,128)S(1)}, f32[32,64]{1,0:T(8,128)S(1)}, f32[32,128]{1,0:T(8,128)S(1)}, f32[320,128]{1,0:T(8,128)S(1)}) custom-call(bf16[64,2048]{1,0:T(8,128)(2,1)} %sig_hbm.1, bf16[16,64,64]{2,1,0:T(8,128)(2,1)} %ret_hbm.1, bf16[32,2,16,2048]{3,2,1,0:T(8,128)(2,1)} %bitcast.15, bf16[320,32,128]{2,1,0:T(8,128)(2,1)} %bitcast.16, ...), custom_call_target="tpu_custom_call" | custom-call | tf_op jit(solution)/shard_map/pallas_call | solution.py:493
  30.6 2.5 %shard_map.141 = (f32[10240,128]{1,0:T(8,128)}, f32[32,64]{1,0:T(8,128)}) custom-call(f32[10560,128]{1,0:T(8,128)S(1)} %get-tuple-element.8.base_ref, f32[32,128]{1,0:T(8,128)S(1)} %get-tuple-element.9.es_ref, f32[320,128]{1,0:T(8,128)S(1)} %get-tuple-element.10.prof_ref, f32[32,64]{1,0:T(8,128)S(1)} %get-tuple-element.11.obs_in), custom_call_target="tpu_custom_call" | custom-call | tf_op jit(solution)/shard_map/pallas_call | solution.py:564

commit v4 on v3

--- a/solution.py
+++ b/solution.py
@@ -12,6 +12,7 @@
 ANY = pl.BlockSpec(memory_space=pl.ANY)
 VM = pl.BlockSpec(memory_space=pltpu.VMEM)
 FINISH = 10
+GREETED = 2
 ROWS = 32
 PITCH = 33
 FACE_PITCH = 9
@@ -58,32 +59,36 @@
     sig, ret, rad, st, lift, vol, exp, target,
     d0, d1, g0, g1, part, recv_a, send_b, recv_b, sens, own_f, other_f,
     rhs, lf, az_send, az_recv, ax_recv, axf, oh_lo, tcol,
-    taper_ref, wobs_ref, wsam_ref, host_ref, prof_ref, relay,
+    taper_ref, wobs_ref, wsam_ref, host_ref, prof_ref, relay, first,
     ld, sa, ra, sb, rb, sc, rc, sp, rp, hx_s, hx_r, ha_s, ha_r, rel_s, rel_r,
 ):
     s = lax.axis_index("stream")
     a = lax.axis_index("azim")
-    core = s % 2
     z_lo = s // 2
-    xy = a % 16
+    core = s - z_lo * 2
     z_hi = a // 16
-    cx, cy = xy // 4, xy % 4
+    xy = a - z_hi * 16
+    cx = xy // 4
+    cy = xy - cx * 4
     q_me = core * 16 + xy
     z_me = z_hi * 4 + z_lo
     steps = peers_by_distance()
 
+    xs = [lax.rem(cx + d, 4) for d in range(4)]
+    ys = [lax.rem(cy + d, 4) for d in range(4)]
+    cs = [core, 1 - core]
+    zs = [lax.rem(z_me + d, 8) for d in range(8)]
+    own_z, own_half = z_lo * 2, z_hi * 16
+
     def group_peer(step):
         dx, dy, dc = step
-        return z_lo * 2 + (core + dc) % 2, z_hi * 16 + ((cx + dx) % 4) * 4 + (cy + dy) % 4
+        return own_z + cs[dc], own_half + xs[dx] * 4 + ys[dy]
 
     def z_peer(dz):
-        z = (z_me + dz) % 8
-        return (z % 4) * 2 + core, (z // 4) * 16 + xy
-
-    def q_of(peer):
-        return (peer[0] % 2) * 16 + peer[1] % 16
-
-    a_next, a_prev = (a + 1) % 32, (a + 31) % 32
+        half = zs[dz] // 4
+        return (zs[dz] - half * 4) * 2 + core, half * 16 + xy
+
+    a_next, a_prev = lax.rem(a + 1, 32), lax.rem(a + 31, 32)
 
     loads = {}
 
@@ -149,9 +154,9 @@
     for k in RELAYS[0] + RELAYS[1]:
         extra = extra + jnp.where(xy == k, 1, 0)
 
-    def send_partial(peer):
+    def send_partial(q, peer):
         pltpu.make_async_remote_copy(
-            src_ref=part.at[q_of(peer)], dst_ref=recv_a.at[q_me], send_sem=sa, recv_sem=ra,
+            src_ref=part.at[q], dst_ref=recv_a.at[q_me], send_sem=sa, recv_sem=ra,
             device_id=peer, device_id_type=MESH,
         ).start()
 
@@ -161,21 +166,24 @@
         acc = dot(rad[q0 : q0 + 8, 0].reshape(128, 2048), d0[...], NT)
         acc = acc + dot(rad[q0 : q0 + 8, 1].reshape(128, 2048), d1[...], NT)
         part[q0 : q0 + 8] = acc.reshape(8, 16, 128).astype(BF)
-        if g == 0:
-            pl.semaphore_wait(barrier, 40 + extra)
         if g == 2:
             load_rest()
-        for dx in (1, 0):
-            for dy in (2, 1, 3, 0):
-                px, py = (g % 2) * 2 + (cx + dx) % 2, (cy + dy) % 4
-                peer = (z_lo * 2 + g // 2, z_hi * 16 + px * 4 + py)
-                if dy != 0:
-                    send_partial(peer)
-                else:
-
-                    @pl.when(q_of(peer) != q_me)
-                    def _():
-                        send_partial(peer)
+        if g == GREETED:
+            pl.semaphore_wait(barrier, 40 + extra)
+        for t in range(g + 1) if g == GREETED else [g] if g > GREETED else []:
+            px = [(t % 2) * 2 + lax.rem(cx + dx, 2) for dx in range(2)]
+            for dx in (1, 0):
+                for dy in (2, 1, 3, 0):
+                    q = px[dx] * 4 + ys[dy]
+                    peer = (own_z + t // 2, own_half + q)
+                    q = q + (t // 2) * 16
+                    if dy != 0:
+                        send_partial(q, peer)
+                    else:
+
+                        @pl.when(q != q_me)
+                        def _():
+                            send_partial(q, peer)
 
     @pl.when(s < 7)
     def _():
@@ -212,8 +220,8 @@
             last = sf[pl.ds(x * 8 + rhi * 4 + 3, 320, stride=PITCH), :].reshape(10, 2, 2, 8, 128)
             packed = jnp.concatenate([last[:, 0, 1, 4:8], last[:, 1, 1, 4:8]], axis=1)
             az_send[0, :, pl.ds(col, 128)] = packed.reshape(80, 128).astype(BF)
-            first = sf[pl.ds(x * 8 + rhi * 4, 320, stride=PITCH), :].reshape(10, 2, 2, 8, 128)
-            packed = jnp.concatenate([first[:, 0, 0, 0:4], first[:, 1, 0, 0:4]], axis=1)
+            head = sf[pl.ds(x * 8 + rhi * 4, 320, stride=PITCH), :].reshape(10, 2, 2, 8, 128)
+            packed = jnp.concatenate([head[:, 0, 0, 0:4], head[:, 1, 0, 0:4]], axis=1)
             az_send[1, :, pl.ds(col, 128)] = packed.reshape(80, 128).astype(BF)
 
     def az_copy(way, dst):
@@ -231,9 +239,9 @@
                     src_ref=az_send.at[way, pl.ds(16 * i + 16, 16)], dst_ref=relay,
                     send_sem=ha_s.at[way], recv_sem=rel_r,
                     device_id=(s, z_hi * 16 + k), device_id_type=MESH).start()
-            first = pl.ds(0, 16)
+            piece = pl.ds(0, 16)
             pltpu.make_async_remote_copy(
-                src_ref=az_send.at[way, first], dst_ref=az_recv.at[way, first],
+                src_ref=az_send.at[way, piece], dst_ref=az_recv.at[way, piece],
                 send_sem=ha_s.at[way], recv_sem=ha_r.at[way],
                 device_id=(s, dst), device_id_type=MESH).start()
 
@@ -371,7 +379,8 @@
     sens[q_me] = own.astype(BF)
     for step in steps:
         pltpu.make_async_remote_copy(
-            src_ref=sens.at[q_me], dst_ref=sens.at[q_me], send_sem=sc, recv_sem=rc,
+            src_ref=sens.at[q_me], dst_ref=sens.at[q_me], send_sem=sc,
+            recv_sem=rc.at[0 if step[0] in (0, 3) else 1],
             device_id=group_peer(step), device_id_type=MESH,
         ).start()
     swap = pltpu.make_async_remote_copy(
@@ -412,21 +421,31 @@
     def _(i):
         sector_row(i * 3)
 
-    pltpu.make_async_copy(sens.at[pl.ds(0, 31)], sens.at[pl.ds(0, 31)], rc).wait()
-    flat = sens[...].reshape(512, 128)
-    h_low = []
-    for g in (g0, g1):
-        h = dot(g[...], flat, NT)
-        h_low.append(jnp.concatenate(halves(h[0:16] + h[16:32]), axis=0))
+    def strengths(group):
+        blocks = [c * 16 + xs[2 * group + d] * 4 for d in range(2) for c in range(2)]
+        flat = jnp.concatenate([sens[pl.ds(q, 4)].reshape(64, 128) for q in blocks], axis=0)
+        low = []
+        for g in (g0, g1):
+            h = dot(g[...], flat, NT)
+            low.append(jnp.concatenate(halves(h[0:16] + h[16:32]), axis=0))
+        for n in range(4):
+            cols = slice(n * 512, n * 512 + 512)
+            val = 0.0
+            for half in range(2):
+                weights = [rad[pl.ds(q, 4), half, :, cols].reshape(64, 512) for q in blocks]
+                val = val + dot(low[half], jnp.concatenate(weights, axis=0))
+            yield cols, val
+
+    pltpu.make_async_copy(sens.at[pl.ds(0, 15)], sens.at[pl.ds(0, 15)], rc.at[0]).wait()
+    for cols, val in strengths(0):
+        first[:, cols] = val
+    pltpu.make_async_copy(sens.at[pl.ds(0, 16)], sens.at[pl.ds(0, 16)], rc.at[1]).wait()
     block_of = lax.broadcasted_iota(jnp.int32, (32, 512), 0) % 16
+    rows = lax.broadcasted_iota(jnp.int32, (32, 512), 0)
     es = jnp.zeros((64, 128), F32)
-    for n in range(4):
-        cols = slice(n * 512, n * 512 + 512)
-        val = dot(h_low[0], rad[:, 0, :, cols].reshape(512, 512))
-        val = val + dot(h_low[1], rad[:, 1, :, cols].reshape(512, 512))
+    for n, (cols, val) in enumerate(strengths(1)):
         mine = lax.broadcasted_iota(jnp.int32, (32, 512), 1) // 128 + n * 4 == block_of
-        strength = jnp.sum(jnp.where(mine, val, 0.0), axis=0, keepdims=True)
-        rows = lax.broadcasted_iota(jnp.int32, (32, 512), 0)
+        strength = jnp.sum(jnp.where(mine, first[:, cols] + val, 0.0), axis=0, keepdims=True)
         spread_rows = jnp.where(rows == point_row[:, cols], strength, 0.0)
         pieces = jnp.concatenate(halves(spread_rows), axis=0)
         es = es + dot(pieces, oh_lo[:, cols], NT)
@@ -534,8 +553,9 @@
             pltpu.VMEM((1, 2048), jnp.int32),
             pltpu.VMEM((320,), F32),
             pltpu.VMEM((16, 1024), BF),
+            pltpu.VMEM((32, 2048), F32),
             dma((16,)),
-            dma, dma, dma, dma, dma, dma, dma, dma,
+            dma, dma, dma, dma, dma, dma((2,)), dma, dma,
             dma((2,)), dma((2,)), dma((2,)), dma((2,)), dma, dma,
         ],
         compiler_params=pltpu.CompilerParams(

time: 33.1 us -> 31.8 us (0.961)
  Pallas kernels: 32.4 us -> 31.1 us
    pallas_call x1, Pallas kernels: 29.9 us -> 28.6 us  [body(): pl.pallas_call(kernel, out_shape=(pltpu.VMEM((320 * PITCH, 128), F32), ja...]
where the time goes in v4:
time: 31.8 us; the launch traced here: 31.7 us
  Pallas kernels  31.1 us (98%)
  between operations  0.64 us (2%)
    pallas_call x1, Pallas kernels, body(): pl.pallas_call(kernel, out_shape=(pltpu.VMEM((320 * PITCH, 128), F32), ja...  28.6 us
    pallas_call x1, Pallas kernels, body(): pl.pallas_call(finish, out_shape=(jax.ShapeDtypeStruct((10240, 128), F32)...  2.48 us

profile of v4, /device:TPU:1, one launch (start us, length us, event | category | flops | bytes accessed | tf_op | source)
XLA Modules:
  0.0 31.7 jit_solution(7905348738904756595)
XLA Ops:
  0.6 28.6 %shard_map.140 = (f32[10560,128]{1,0:T(8,128)S(1)}, f32[32,64]{1,0:T(8,128)S(1)}, f32[32,128]{1,0:T(8,128)S(1)}, f32[320,128]{1,0:T(8,128)S(1)}) custom-call(bf16[64,2048]{1,0:T(8,128)(2,1)} %sig_hbm.1, bf16[16,64,64]{2,1,0:T(8,128)(2,1)} %ret_hbm.1, bf16[32,2,16,2048]{3,2,1,0:T(8,128)(2,1)} %bitcast.15, bf16[320,32,128]{2,1,0:T(8,128)(2,1)} %bitcast.16, ...), custom_call_target="tpu_custom_call" | custom-call | tf_op jit(solution)/shard_map/pallas_call | solution.py:512
  29.3 2.5 %shard_map.141 = (f32[10240,128]{1,0:T(8,128)}, f32[32,64]{1,0:T(8,128)}) custom-call(f32[10560,128]{1,0:T(8,128)S(1)} %get-tuple-element.8.base_ref, f32[32,128]{1,0:T(8,128)S(1)} %get-tuple-element.9.es_ref, f32[320,128]{1,0:T(8,128)S(1)} %get-tuple-element.10.prof_ref, f32[32,64]{1,0:T(8,128)S(1)} %get-tuple-element.11.obs_in), custom_call_target="tpu_custom_call" | custom-call | tf_op jit(solution)/shard_map/pallas_call | solution.py:584

commit v5 on v4

--- a/solution.py
+++ b/solution.py
@@ -118,12 +118,21 @@
     def greet(peer):
         pl.semaphore_signal(barrier, inc=1, device_id=peer, device_id_type=MESH)
 
-    for step in steps:
+    ends = (15, 0)
+    for way in range(2):
+
+        @pl.when(xy == ends[1 - way])
+        def _():
+            for k in RELAYS[way]:
+                greet((s, (1 - z_hi) * 16 + k))
+
+    greet(z_peer(4))
+    for step in steps[:2]:
         greet(group_peer(step))
-    for dz in range(1, 8):
-        greet(z_peer(dz))
     greet((s, a_next))
     greet((s, a_prev))
+    for dz in (3, 5):
+        greet(z_peer(dz))
 
     @pl.when(s > 0)
     def _():
@@ -133,13 +142,10 @@
     def _():
         greet((s + 1, a))
 
-    ends = (15, 0)
-    for way in range(2):
-        for k in RELAYS[way]:
-
-            @pl.when(xy == ends[1 - way])
-            def _():
-                greet((s, (1 - z_hi) * 16 + k))
+    for step in steps[2:]:
+        greet(group_peer(step))
+    for dz in (2, 6, 1, 7):
+        greet(z_peer(dz))
 
     loads[0].wait()
     loads[1].wait()

time: 31.8 us -> 31.6 us (level)
  no operation moved by 1% of the time
where the time goes in v5:
time: 31.6 us; the launch traced here: 31.5 us
  Pallas kernels  30.8 us (97%)
  between operations  0.64 us (2%)
    pallas_call x1, Pallas kernels, body(): pl.pallas_call(kernel, out_shape=(pltpu.VMEM((320 * PITCH, 128), F32), ja...  28.4 us
    pallas_call x1, Pallas kernels, body(): pl.pallas_call(finish, out_shape=(jax.ShapeDtypeStruct((10240, 128), F32)...  2.48 us

profile of v5, /device:TPU:1, one launch (start us, length us, event | category | flops | bytes accessed | tf_op | source)
XLA Modules:
  0.0 31.5 jit_solution(16287853523109314194)
XLA Ops:
  0.6 28.4 %shard_map.140 = (f32[10560,128]{1,0:T(8,128)S(1)}, f32[32,64]{1,0:T(8,128)S(1)}, f32[32,128]{1,0:T(8,128)S(1)}, f32[320,128]{1,0:T(8,128)S(1)}) custom-call(bf16[64,2048]{1,0:T(8,128)(2,1)} %sig_hbm.1, bf16[16,64,64]{2,1,0:T(8,128)(2,1)} %ret_hbm.1, bf16[32,2,16,2048]{3,2,1,0:T(8,128)(2,1)} %bitcast.15, bf16[320,32,128]{2,1,0:T(8,128)(2,1)} %bitcast.16, ...), custom_call_target="tpu_custom_call" | custom-call | tf_op jit(solution)/shard_map/pallas_call | solution.py:518
  29.0 2.5 %shard_map.141 = (f32[10240,128]{1,0:T(8,128)}, f32[32,64]{1,0:T(8,128)}) custom-call(f32[10560,128]{1,0:T(8,128)S(1)} %get-tuple-element.8.base_ref, f32[32,128]{1,0:T(8,128)S(1)} %get-tuple-element.9.es_ref, f32[320,128]{1,0:T(8,128)S(1)} %get-tuple-element.10.prof_ref, f32[32,64]{1,0:T(8,128)S(1)} %get-tuple-element.11.obs_in), custom_call_target="tpu_custom_call" | custom-call | tf_op jit(solution)/shard_map/pallas_call | solution.py:590

commit v6 on v5

--- a/solution.py
+++ b/solution.py
@@ -383,10 +383,10 @@
     own = weight_own * (total - target_own)
     own_f[...] = own
     sens[q_me] = own.astype(BF)
-    for step in steps:
+    for step in sorted(steps, key=lambda t: t[2]):
         pltpu.make_async_remote_copy(
             src_ref=sens.at[q_me], dst_ref=sens.at[q_me], send_sem=sc,
-            recv_sem=rc.at[0 if step[0] in (0, 3) else 1],
+            recv_sem=rc.at[step[2]],
             device_id=group_peer(step), device_id_type=MESH,
         ).start()
     swap = pltpu.make_async_remote_copy(
@@ -428,8 +428,8 @@
         sector_row(i * 3)
 
     def strengths(group):
-        blocks = [c * 16 + xs[2 * group + d] * 4 for d in range(2) for c in range(2)]
-        flat = jnp.concatenate([sens[pl.ds(q, 4)].reshape(64, 128) for q in blocks], axis=0)
+        chunks = pl.ds(cs[group] * 16, 16)
+        flat = sens[chunks].reshape(256, 128)
         low = []
         for g in (g0, g1):
             h = dot(g[...], flat, NT)
@@ -438,8 +438,7 @@
             cols = slice(n * 512, n * 512 + 512)
             val = 0.0
             for half in range(2):
-                weights = [rad[pl.ds(q, 4), half, :, cols].reshape(64, 512) for q in blocks]
-                val = val + dot(low[half], jnp.concatenate(weights, axis=0))
+                val = val + dot(low[half], rad[chunks, half, :, cols].reshape(256, 512))
             yield cols, val
 
     pltpu.make_async_copy(sens.at[pl.ds(0, 15)], sens.at[pl.ds(0, 15)], rc.at[0]).wait()

time: 31.6 us -> 31.5 us (level)
  no operation moved by 1% of the time
where the time goes in v6:
time: 31.5 us
  Pallas kernels  30.8 us (98%)
  between operations  0.64 us (2%)
    pallas_call x1, Pallas kernels, body(): pl.pallas_call(kernel, out_shape=(pltpu.VMEM((320 * PITCH, 128), F32), ja...  28.3 us
    pallas_call x1, Pallas kernels, body(): pl.pallas_call(finish, out_shape=(jax.ShapeDtypeStruct((10240, 128), F32)...  2.48 us

profile of v6, /device:TPU:1, one launch (start us, length us, event | category | flops | bytes accessed | tf_op | source)
XLA Modules:
  0.0 31.5 jit_solution(363989993650104721)
XLA Ops:
  0.6 28.3 %shard_map.140 = (f32[10560,128]{1,0:T(8,128)S(1)}, f32[32,64]{1,0:T(8,128)S(1)}, f32[32,128]{1,0:T(8,128)S(1)}, f32[320,128]{1,0:T(8,128)S(1)}) custom-call(bf16[64,2048]{1,0:T(8,128)(2,1)} %sig_hbm.1, bf16[16,64,64]{2,1,0:T(8,128)(2,1)} %ret_hbm.1, bf16[32,2,16,2048]{3,2,1,0:T(8,128)(2,1)} %bitcast.15, bf16[320,32,128]{2,1,0:T(8,128)(2,1)} %bitcast.16, ...), custom_call_target="tpu_custom_call" | custom-call | tf_op jit(solution)/shard_map/pallas_call | solution.py:517
  29.0 2.5 %shard_map.141 = (f32[10240,128]{1,0:T(8,128)}, f32[32,64]{1,0:T(8,128)}) custom-call(f32[10560,128]{1,0:T(8,128)S(1)} %get-tuple-element.8.base_ref, f32[32,128]{1,0:T(8,128)S(1)} %get-tuple-element.9.es_ref, f32[320,128]{1,0:T(8,128)S(1)} %get-tuple-element.10.prof_ref, f32[32,64]{1,0:T(8,128)S(1)} %get-tuple-element.11.obs_in), custom_call_target="tpu_custom_call" | custom-call | tf_op jit(solution)/shard_map/pallas_call | solution.py:589
